TPU v7x, 1024 devices: a whole 8x8x8 slice. The times are simulated.
1024 devices in a mesh: ctx: 64 (over x, z), head: 16 (over y, core).
Axes of the slice: x: 8, y: 8, z: 8, core: 2. Of those that a mesh axis runs over, the one named last changes fastest.
Arguments:
- acts: bfloat16 [32768, 4096], P('ctx'), may hold values from -16 to 16
- queries: bfloat16 [32768, 4096], P('ctx', 'head'), may hold values from -6 to 6
- keys: bfloat16 [32768, 4096], P('ctx', 'head'), may hold values from -6 to 6
- values: bfloat16 [32768, 4096], P('ctx', 'head'), may hold values from -6 to 6
- out_grad: bfloat16 [32768, 4096], P('ctx', 'head'), may hold values from -6 to 6
Outputs:
- q_grad: bfloat16 [32768, 4096], P('ctx', 'head')
- k_grad: bfloat16 [32768, 4096], P('ctx', 'head')
- v_grad: bfloat16 [32768, 4096], P('ctx', 'head')
- wv_grad: float32 [4096, 4096], P('ctx', 'head')
All inputs are finite; a program needn't handle non-finite values.
Results may differ from a plain program's by a relative error of at most 0.0064.
Values may be sent and summed in bfloat16 or wider, within the bound.
No kernel may reach another device: no remote copies, remote signals or barrier semaphores. Data moves between devices by JAX's collectives and lax.ppermute only.
A program may use at most 64 MiB of HBM per device.

v0:
```python
import jax
import jax.numpy as jnp
from jax import lax
from jax.sharding import Mesh
from jax.sharding import PartitionSpec as P

DH = 128
CTX = ("ctx_0", "ctx_1")


def summed_rows(so_far, axes):
    for axis in axes:
        so_far = lax.psum_scatter(so_far, axis, scatter_dimension=0, tiled=True)
    return so_far


def normalize(block):
    full = block.astype(jnp.float32)
    factor = lax.rsqrt(jnp.sum(full * full, axis=-1, keepdims=True) + 1e-06)
    unit = full * factor
    return (unit, unit.astype(jnp.bfloat16), factor)


def project_back(unit, factor, grad_unit):
    inner = jnp.sum(unit * grad_unit, axis=-1, keepdims=True)
    return (factor * (grad_unit - unit * inner)).astype(jnp.bfloat16)


def scatter_weights(acts, dv_out):
    return summed_rows(
        lax.dot_general(acts, dv_out, (((0,), (0,)), ((), ())), preferred_element_type=jnp.float32),
        CTX,
    )


def on_device(acts, queries, keys, values, out_grad):
    tok_rows = queries.shape[0]
    local_heads = queries.shape[1] // DH
    shape_three = (tok_rows, local_heads, DH)
    q_unit, q_low, q_factor = normalize(queries.reshape(shape_three))
    k_unit, k_low, k_factor = normalize(keys.reshape(shape_three))
    val_block = values.reshape(shape_three)
    grad_block = out_grad.reshape(shape_three)
    nblocks = lax.axis_size(CTX)
    score_scale = float(tok_rows * nblocks) ** (-0.5)
    kv_local = jnp.einsum("tha,thc->hac", k_low, val_block, preferred_element_type=jnp.float32)
    g_local = jnp.einsum("tha,thc->hac", q_low, grad_block, preferred_element_type=jnp.float32)
    state_len = local_heads * DH * DH
    stacked = jnp.stack((kv_local.reshape(state_len), g_local.reshape(state_len)), 0)
    received = lax.all_to_all(stacked, CTX, split_axis=1, concat_axis=0, tiled=True)
    piece_len = state_len // nblocks
    received = received.reshape(nblocks, 2, piece_len)
    kv_part = received[:, 0]
    g_part = received[:, 1]
    kv_before = jnp.cumsum(kv_part, axis=0) - kv_part
    g_after = jnp.flip(jnp.cumsum(jnp.flip(g_part, 0), axis=0), 0) - g_part
    answers = (
        jnp.stack((kv_before, g_after), 1).reshape(nblocks * 2, piece_len).astype(jnp.bfloat16)
    )
    returned = lax.all_to_all(answers, CTX, split_axis=0, concat_axis=1, tiled=True)
    kv_low = returned[0].reshape(local_heads, DH, DH)
    g_low = returned[1].reshape(local_heads, DH, DH)
    causal_mask = jnp.tril(jnp.ones((tok_rows, tok_rows), dtype=bool))
    grad_scores = jnp.einsum(
        "thc,shc->hts", grad_block, val_block, preferred_element_type=jnp.float32
    )
    grad_scores = jnp.where(causal_mask[None], grad_scores * score_scale, 0.0).astype(jnp.bfloat16)
    dqn = jnp.einsum("hts,sha->tha", grad_scores, k_low, preferred_element_type=jnp.float32)
    dqn = dqn + score_scale * jnp.einsum(
        "thc,hac->tha", grad_block, kv_low, preferred_element_type=jnp.float32
    )
    dkn = jnp.einsum("hst,sha->tha", grad_scores, q_low, preferred_element_type=jnp.float32)
    dkn = dkn + score_scale * jnp.einsum(
        "thc,hac->tha", val_block, g_low, preferred_element_type=jnp.float32
    )
    dq_out = project_back(q_unit, q_factor, dqn).reshape(tok_rows, local_heads * DH)
    dk_out = project_back(k_unit, k_factor, dkn).reshape(tok_rows, local_heads * DH)
    dq_out, dk_out = (dq_out, dk_out)
    attn = jnp.einsum("tha,sha->hts", q_low, k_low, preferred_element_type=jnp.float32)
    attn = jnp.where(causal_mask[None], attn * score_scale, 0.0).astype(jnp.bfloat16)
    dvv = jnp.einsum("hst,shc->thc", attn, grad_block, preferred_element_type=jnp.float32)
    dvv = dvv + score_scale * jnp.einsum(
        "tha,hac->thc", k_low, g_low, preferred_element_type=jnp.float32
    )
    dv_out = dvv.astype(jnp.bfloat16).reshape(tok_rows, local_heads * DH)
    wv_grad = scatter_weights(acts, dv_out)
    return (dq_out, dk_out, dv_out, wv_grad)


def solution(mesh):
    finer = Mesh(mesh.devices.reshape(8, 8, mesh.shape["head"]), ("ctx_0", "ctx_1", "head"))
    return jax.shard_map(
        on_device,
        mesh=finer,
        in_specs=(P(CTX, None), P(CTX, "head"), P(CTX, "head"), P(CTX, "head"), P(CTX, "head")),
        out_specs=(P(CTX, "head"), P(CTX, "head"), P(CTX, "head"), P(CTX, "head")),
        check_vma=False,
    )
```

profile of v0, /device:TPU:6, one launch (start us, length us, event | category | flops | bytes accessed | tf_op | source)
XLA Modules:
  0.0 183.1 jit_solution(1801775788466893134)
XLA Ops:
  7.2 0.0 copy-start
  7.2 1.1 copy.71
  8.3 1.1 copy.44
  9.4 0.1 multiply_reduce_fusion.1
  9.5 1.1 copy.45
  10.6 0.1 multiply_reduce_fusion
  10.7 0.1 multiply_convert_fusion
  10.8 0.2 fusion.38
  11.0 0.0 copy-done
  11.0 0.2 fusion.25
  11.3 0.2 pad_maximum_fusion
  11.5 35.6 %all_to_all.26 = f32[2,64,512]{2,0,1:T(2,128)S(1)} all-to-all(f32[2,64,512]{2,0,1:T(2,128)S(1)} %pad_maximum_fusion), channel_id=1, replica_groups=mesh['ctx_0'=8,'ctx_1'=8,'head'=16] {'ctx_0','ctx_1'}, dimensions={1} | all-to-all | bytes 524288 | tf_op jit(solution)/shard_map/all_to_all | solution.py:50
  47.1 0.1 fusion.33
  47.2 0.2 subtract_convert_fusion.1
  47.5 0.1 rev.7
  47.6 0.1 reduce_window_sum.18
  47.7 0.1 rev.8
  47.9 0.1 copy.52
  48.0 1.0 pad_maximum_fusion.1
  49.0 6.4 %all-to-all-start.1 = ((bf16[64,2,512]{2,1,0:T(2,128)(2,1)}), bf16[64,2,512]{2,1,0:T(2,128)(2,1)S(1)}, u32[]{:S(2)}, u32[]{:S(2)}) async-start(bf16[64,2,512]{2,1,0:T(2,128)(2,1)} %pad_maximum_fusion.1), calls=%async_computation.1 | async-start | bytes 262144 | tf_op jit(solution)/shard_map/all_to_all | solution.py:60
  55.4 0.0 reduce-scatter.5.cloned.1.call-start
  55.4 0.1 iota_compare_fusion
  55.5 0.0 copy-start.1
  55.5 10.2 %all-to-all-done.1 = bf16[64,2,512]{2,1,0:T(2,128)(2,1)S(1)} async-done(((bf16[64,2,512]{2,1,0:T(2,128)(2,1)}), bf16[64,2,512]{2,1,0:T(2,128)(2,1)S(1)}, u32[]{:S(2)}, u32[]{:S(2)}) %all-to-all-start.1) | async-done | bytes 131104 | tf_op jit(solution)/shard_map/all_to_all | solution.py:60
  65.7 0.5 slice_reduce_fusion
  66.3 0.1 reshape_squeeze.7
  66.3 0.3 fusion.13
  66.6 0.7 fusion.16
  67.3 0.0 copy-done.1
  67.4 5.4 %convolution_bitcast_fusion = f32[4096,256]{0,1:T(8,128)} fusion(bf16[512,256]{0,1:T(8,128)(2,1)S(1)} %bitcast.81, bf16[512,4096]{1,0:T(8,128)(2,1)} %param.5), kind=kOutput, calls=%fused_computation.2 | convolution fusion | flops 1073741824 | bytes 8650752 | tf_op jit(solution)/shard_map/dot_general | solution.py:31
  72.7 0.0 reduce-scatter.5.cloned.1.call-update
  72.8 0.0 reduce-scatter.7.cloned.1.call-start
  72.8 1.5 select_convert_fusion.1
  74.4 1.1 convolution_multiply_fusion.1
  75.4 51.9 %reduce-scatter.5.cloned.1.call-done = f32[512,256]{0,1:T(8,128)} async-done(((f32[4096,256]{0,1:T(8,128)}), f32[512,256]{0,1:T(8,128)}) %reduce-scatter.5.cloned.1.call-update) | async-done | bytes 524304 | tf_op jit(solution)/shard_map/reduce_scatter | solution.py:13
  127.3 2.0 %copy.68 = f32[512,256]{1,0:T(8,128)} copy(f32[512,256]{0,1:T(8,128)} %reduce-scatter.5.cloned.1.call-done) | data formatting | bytes 1048576
  129.4 0.0 reduce-scatter.7.cloned.1.call-update
  129.4 2.2 %fusion.3 = f32[512,2,128]{0,2,1:T(8,128)} fusion(f32[2,128,512]{2,1,0:T(8,128)} %convolution_multiply_fusion.1, bf16[512,2,128]{0,2,1:T(8,128)(2,1)S(1)} %get-tuple-element.20, bf16[2,512,512]{2,1,0:T(8,128)(2,1)S(1)} %select_convert_fusion.1), kind=kOutput, calls=%fused_computation.7 | convolution fusion | flops 134348800 | bytes 2359296 | tf_op jit(solution)/shard_map/hst,sha->tha/dot_general | solution.py:72
  131.6 0.8 copy.62
  132.4 0.1 reshape_squeeze.6
  132.5 1.4 fusion.14
  133.8 0.8 copy.61
  134.7 0.2 convolution_multiply_fusion.2
  134.9 0.5 fusion.4
  135.4 0.2 fusion.15
  135.5 0.8 copy.60
  136.4 39.9 %reduce-scatter.7.cloned.1.call-done = f32[64,256]{1,0:T(8,128)} async-done(((f32[512,256]{1,0:T(8,128)}), f32[64,256]{1,0:T(8,128)}) %reduce-scatter.7.cloned.1.call-update) | async-done | bytes 65552
  (4 shorter events, 0.0 us)
Async XLA Ops:
  7.2 3.9 %copy-start = (bf16[512,256]{1,0:T(8,128)(2,1)S(1)}, bf16[512,256]{1,0:T(8,128)(2,1)}, u32[]{:S(2)}) copy-start(bf16[512,256]{1,0:T(8,128)(2,1)} %param.8) | copy-start | bytes 786436
  49.0 16.8 %all-to-all-start.1 = ((bf16[64,2,512]{2,1,0:T(2,128)(2,1)}), bf16[64,2,512]{2,1,0:T(2,128)(2,1)S(1)}, u32[]{:S(2)}, u32[]{:S(2)}) async-start(bf16[64,2,512]{2,1,0:T(2,128)(2,1)} %pad_maximum_fusion.1), calls=%async_computation.1 | async-start | bytes 262144 | tf_op jit(solution)/shard_map/all_to_all | solution.py:60
  55.4 72.0 %reduce-scatter.5.cloned.1.call-start = ((), (), s32[]{:S(2)}) async-start(), calls=%async_computation.4 | async-start | bytes 4718592 | tf_op jit(solution)/shard_map/reduce_scatter | solution.py:13
  55.5 11.8 %copy-start.1 = (pred[512,512]{1,0:T(8,128)(4,1)}, pred[512,512]{1,0:T(8,128)(4,1)S(1)}, u32[]{:S(2)}) copy-start(pred[512,512]{1,0:T(8,128)(4,1)S(1)} %iota_compare_fusion) | copy-start | bytes 786436
  72.8 103.5 %reduce-scatter.7.cloned.1.call-start = ((), (), s32[]{:S(2)}) async-start(), calls=%async_computation.5 | async-start | bytes 589824
Sparse Core Ops, SparseCore 0:
  72.9 54.4 reduce-scatter.4
  131.3 44.9 reduce-scatter.6
where the time goes:
time: 184 us; the launch traced here: 183 us
  waiting for transfers between devices  102 us (55%)
  blocking collectives  35.6 us (19%)
  between operations  14.3 us (8%)
  matrix products  12.3 us (7%)
  local copies, waits for them, and re-layouts  8.85 us (5%)
  starting transfers between devices  6.49 us (4%)
  other arithmetic  3.56 us (2%)
    reduce_scatter x1, waiting for transfers between devices, summed_rows(): so_far = lax.psum_scatter(so_far, axis, scatter_dimension=0, tiled=True)  51.9 us
    unnamed x3, waiting for transfers between devices  40 us
    all_to_all x1, blocking collectives, on_device(): lax.all_to_all(stacked, CTX, split_axis=1, concat_axis=0, tiled=True)  35.6 us
    all_to_all x1, waiting for transfers between devices, on_device(): lax.all_to_all(answers, CTX, split_axis=0, concat_axis=1, tiled=True)  10.2 us
    all_to_all x1, starting transfers between devices, on_device(): lax.all_to_all(answers, CTX, split_axis=0, concat_axis=1, tiled=True)  6.41 us
    dot_general x1, matrix products, scatter_weights(): lax.dot_general(acts, dv_out, (((0,), (0,)), ((), ())), preferred_element...  5.37 us
    unnamed x9, local copies, waits for them, and re-layouts  4.58 us
  transfers between devices with their start and end apart: 3, of which 3 were waited for; matrix products, arithmetic and copies ran while one was open for 5% of the time, Pallas kernels for 0%

commit v1 on v0

v1 whole, which is shorter than its diff:
```python
import functools

import jax
import jax.numpy as jnp
from jax import lax
from jax.experimental import pallas as pl
from jax.experimental.pallas import tpu as pltpu
from jax.sharding import Mesh
from jax.sharding import PartitionSpec as P

DH = 128
CTX = ("ctx_0", "ctx_1")
F32 = jnp.float32
BF16 = jnp.bfloat16


def dot(a, b, ca, cb):
    return lax.dot_general(a, b, (((ca,), (cb,)), ((), ())), preferred_element_type=F32)


def unit_of(block):
    full = block.astype(F32)
    factor = lax.rsqrt(jnp.sum(full * full, axis=-1, keepdims=True) + 1e-06)
    return full * factor, factor


def head(ref, h):
    return ref[:, h * DH : (h + 1) * DH]


def states_kernel(q_ref, k_ref, v_ref, o_ref, st_ref):
    heads = q_ref.shape[1] // DH
    rows = DH // 8
    for h in range(heads):
        kn = unit_of(head(k_ref, h))[0].astype(BF16)
        qn = unit_of(head(q_ref, h))[0].astype(BF16)
        kv = dot(kn, head(v_ref, h), 0, 0)
        g = dot(qn, head(o_ref, h), 0, 0)
        st_ref[h * rows : (h + 1) * rows] = kv.reshape(rows, 8, DH).astype(st_ref.dtype)
        at = (heads + h) * rows
        st_ref[at : at + rows] = g.reshape(rows, 8, DH).astype(st_ref.dtype)


def scan_kernel(back_ref, r_ref, out_ref):
    n = r_ref.shape[0]
    back = back_ref[0]

    def step(i, acc):
        b = jnp.where(back == 1, n - 1 - i, i)
        out_ref[b] = acc.astype(out_ref.dtype)
        return acc + r_ref[b].astype(F32)

    lax.fori_loop(0, n, step, jnp.zeros(r_ref.shape[1:], F32), unroll=8)


def local_kernel(scale, q_ref, k_ref, v_ref, o_ref, dq_ref, dk_ref, dv_ref):
    toks, width = q_ref.shape
    mask = lax.broadcasted_iota(jnp.int32, (toks, toks), 0) >= lax.broadcasted_iota(
        jnp.int32, (toks, toks), 1
    )
    for h in range(width // DH):
        at = slice(h * DH, (h + 1) * DH)
        kn = unit_of(head(k_ref, h))[0].astype(BF16)
        qn = unit_of(head(q_ref, h))[0].astype(BF16)
        v, o = head(v_ref, h), head(o_ref, h)
        attn = jnp.where(mask, dot(qn, kn, 1, 1) * scale, 0.0).astype(BF16)
        dv_ref[:, at] = dot(attn, o, 0, 0)
        scores = jnp.where(mask, dot(o, v, 1, 1) * scale, 0.0).astype(BF16)
        dq_ref[:, at] = dot(scores, kn, 1, 0)
        dk_ref[:, at] = dot(scores, qn, 0, 0)


def state(st_ref, kind, h):
    heads = st_ref.shape[0] // 2 // (DH // 8)
    rows = DH // 8
    at = (kind * heads + h) * rows
    return st_ref[at : at + rows].astype(F32).reshape(DH, DH).astype(BF16)


def weights_kernel(scale, acts_ref, k_ref, loc_ref, st_ref, dv_ref, w_ref, dvs_ref):
    @pl.when(pl.program_id(0) == 0)
    def _():
        for h in range(k_ref.shape[1] // DH):
            at = slice(h * DH, (h + 1) * DH)
            kn = unit_of(head(k_ref, h))[0].astype(BF16)
            dvv = loc_ref[:, at] + scale * dot(kn, state(st_ref, 1, h), 1, 0)
            dvs_ref[:, at] = dvv.astype(BF16)
        dv_ref[...] = dvs_ref[...]

    w_ref[...] = dot(acts_ref[...], dvs_ref[...], 0, 0).astype(w_ref.dtype)


def back_kernel(scale, q_ref, k_ref, v_ref, o_ref, lq_ref, lk_ref, st_ref, dq_ref, dk_ref):
    for h in range(q_ref.shape[1] // DH):
        at = slice(h * DH, (h + 1) * DH)
        for src, other, loc, kind, out in (
            (q_ref, o_ref, lq_ref, 0, dq_ref),
            (k_ref, v_ref, lk_ref, 1, dk_ref),
        ):
            unit, factor = unit_of(head(src, h))
            grad = loc[:, at] + scale * dot(head(other, h), state(st_ref, kind, h), 1, 1)
            inner = jnp.sum(unit * grad, axis=-1, keepdims=True)
            out[:, at] = (factor * (grad - unit * inner)).astype(BF16)


def shape(dims, dtype):
    return jax.ShapeDtypeStruct(dims, dtype)


def on_device(acts, queries, keys, values, out_grad):
    toks, width = queries.shape
    nblocks = lax.axis_size(CTX)
    scale = float(toks * nblocks) ** (-0.5)
    pieces = 2 * width // 8
    st = pl.pallas_call(
        states_kernel, out_shape=shape((pieces, 8, DH), BF16), name="states"
    )(queries, keys, values, out_grad)
    received = lax.all_to_all(st, CTX, split_axis=0, concat_axis=0, tiled=True)
    back = (lax.axis_index(CTX) >= nblocks // 2).astype(jnp.int32).reshape(1)
    answers = pl.pallas_call(
        scan_kernel,
        in_specs=[pl.BlockSpec(memory_space=pltpu.SMEM), pl.BlockSpec()],
        out_shape=shape((nblocks, 8, DH), BF16),
        name="scan",
    )(back, received)
    low = lax.all_to_all(answers, CTX, split_axis=0, concat_axis=0, tiled=True)
    part = shape((toks, width), F32)
    lq, lk, lv = pl.pallas_call(
        functools.partial(local_kernel, scale), out_shape=(part, part, part), name="local"
    )(queries, keys, values, out_grad)
    rows = acts.shape[1]
    step = 512
    whole = lambda *dims: pl.BlockSpec(dims, lambda i: (0,) * len(dims))
    dv_out, w = pl.pallas_call(
        functools.partial(weights_kernel, scale),
        grid=(rows // step,),
        in_specs=[
            pl.BlockSpec((toks, step), lambda i: (0, i)),
            whole(toks, width),
            whole(toks, width),
            whole(pieces, 8, DH),
        ],
        out_specs=(whole(toks, width), pl.BlockSpec((step, width), lambda i: (i, 0))),
        out_shape=(shape((toks, width), BF16), shape((rows, width), BF16)),
        scratch_shapes=[pltpu.VMEM((toks, width), BF16)],
        name="weights",
    )(acts, keys, lv, low)
    wv = lax.psum_scatter(w, CTX, scatter_dimension=0, tiled=True)
    dq_out, dk_out = pl.pallas_call(
        functools.partial(back_kernel, scale),
        out_shape=(shape((toks, width), BF16),) * 2,
        name="back",
    )(queries, keys, values, out_grad, lq, lk, low)
    return dq_out, dk_out, dv_out, wv.astype(F32)


def solution(mesh):
    finer = Mesh(mesh.devices.reshape(8, 8, mesh.shape["head"]), ("ctx_0", "ctx_1", "head"))
    return jax.shard_map(
        on_device,
        mesh=finer,
        in_specs=(P(CTX, None), P(CTX, "head"), P(CTX, "head"), P(CTX, "head"), P(CTX, "head")),
        out_specs=(P(CTX, "head"), P(CTX, "head"), P(CTX, "head"), P(CTX, "head")),
        check_vma=False,
    )
```

time: 184 us -> 331 us (1.80)
  the two profiles are of different devices: /device:TPU:6 before, /device:TPU:4 now
where the time goes in v1:
time: 331 us
  waiting for transfers between devices  266 us (80%)
  starting transfers between devices  28.9 us (9%)
  Pallas kernels  19.2 us (6%)
  between operations  14.1 us (4%)
    reduce_scatter x1, waiting for transfers between devices, on_device(): wv = lax.psum_scatter(w, CTX, scatter_dimension=0, tiled=True)  248 us
    all_to_all x1, starting transfers between devices, on_device(): received = lax.all_to_all(st, CTX, split_axis=0, concat_axis=0, tiled=True)  22.7 us
    all_to_all x1, waiting for transfers between devices, on_device(): received = lax.all_to_all(st, CTX, split_axis=0, concat_axis=0, tiled=True)  11.1 us
    pallas_call x1, Pallas kernels, on_device(): pl.pallas_call(functools.partial(weights_kernel, scale), grid=(rows // st...  7.93 us
    all_to_all x1, waiting for transfers between devices, on_device(): low = lax.all_to_all(answers, CTX, split_axis=0, concat_axis=0, tiled=True)  7.08 us
  transfers between devices with their start and end apart: 3, of which 3 were waited for; matrix products, arithmetic and copies ran while one was open for 0% of the time, Pallas kernels for 2%

profile of v1, /device:TPU:4, one launch (start us, length us, event | category | flops | bytes accessed | tf_op | source)
XLA Modules:
  0.0 330.6 jit_solution(1088635639786417895)
XLA Ops:
  7.2 2.5 states.1
  9.7 22.7 %all-to-all-start = ((bf16[64,8,128]{2,1,0:T(8,128)(2,1)}), bf16[64,8,128]{2,1,0:T(8,128)(2,1)S(1)}, u32[]{:S(2)}, u32[]{:S(2)}) async-start(bf16[64,8,128]{2,1,0:T(8,128)(2,1)} %states.1), calls=%async_computation | async-start | bytes 262144 | tf_op jit(solution)/shard_map/all_to_all | solution.py:118
  32.4 11.1 %all-to-all-done.r_ref = bf16[64,8,128]{2,1,0:T(8,128)(2,1)S(1)} async-done(((bf16[64,8,128]{2,1,0:T(8,128)(2,1)}), bf16[64,8,128]{2,1,0:T(8,128)(2,1)S(1)}, u32[]{:S(2)}, u32[]{:S(2)}) %all-to-all-start) | async-done | bytes 131104 | tf_op jit(solution)/shard_map/all_to_all | solution.py:118
  43.5 0.0 copy-start.1
  43.5 0.7 copy-done.1
  44.2 1.7 scan.1
  45.9 6.2 %all-to-all-start.1 = ((bf16[64,8,128]{2,1,0:T(8,128)(2,1)}), bf16[64,8,128]{2,1,0:T(8,128)(2,1)S(1)}, u32[]{:S(2)}, u32[]{:S(2)}) async-start(bf16[64,8,128]{2,1,0:T(8,128)(2,1)} %scan.1), calls=%async_computation.1 | async-start | bytes 262144 | tf_op jit(solution)/shard_map/all_to_all | solution.py:126
  52.0 0.0 reduce-scatter.2.cloned.1.call-start
  52.1 4.0 %local.1 = (f32[512,256]{1,0:T(8,128)}, f32[512,256]{1,0:T(8,128)}, f32[512,256]{1,0:T(8,128)}) custom-call(bf16[512,256]{1,0:T(8,128)(2,1)} %q_ref.5, bf16[512,256]{1,0:T(8,128)(2,1)} %k_ref.7, bf16[512,256]{1,0:T(8,128)(2,1)} %v_ref.5, bf16[512,256]{1,0:T(8,128)(2,1)} %o_ref.5), custom_call_target="tpu_custom_call" | custom-call | tf_op jit(solution)/shard_map/local/pallas_call | solution.py:128
  56.1 7.1 %all-to-all-done.1.st_ref = bf16[64,8,128]{2,1,0:T(8,128)(2,1)S(1)} async-done(((bf16[64,8,128]{2,1,0:T(8,128)(2,1)}), bf16[64,8,128]{2,1,0:T(8,128)(2,1)S(1)}, u32[]{:S(2)}, u32[]{:S(2)}) %all-to-all-start.1) | async-done | bytes 131104 | tf_op jit(solution)/shard_map/all_to_all | solution.py:126
  63.2 0.0 copy-start
  63.2 0.6 copy-done
  63.8 7.9 %weights.1 = (bf16[512,256]{1,0:T(8,128)(2,1)}, bf16[4096,256]{1,0:T(8,128)(2,1)}) custom-call(bf16[512,4096]{1,0:T(8,128)(2,1)} %acts_ref.1, bf16[512,256]{1,0:T(8,128)(2,1)} %k_ref.7, f32[512,256]{1,0:T(8,128)} %get-tuple-element.15.loc_ref, bf16[64,8,128]{2,1,0:T(8,128)(2,1)} %copy-done), custom_call_target="tpu_custom_call" | custom-call | tf_op jit(solution)/shard_map/weights/pallas_call | solution.py:134
  71.8 0.0 reduce-scatter.2.cloned.1.call-update
  71.8 3.0 back.1
  74.8 247.6 %reduce-scatter.2.cloned.1.call-done = bf16[64,256]{1,0:T(8,128)(2,1)} async-done(((bf16[4096,256]{1,0:T(8,128)(2,1)}), bf16[64,256]{1,0:T(8,128)(2,1)}) %reduce-scatter.2.cloned.1.call-update) | async-done | bytes 32784 | tf_op jit(solution)/shard_map/reduce_scatter | solution.py:148
  322.4 1.4 convert_element_type.4
Async XLA Ops:
  9.7 33.8 %all-to-all-start = ((bf16[64,8,128]{2,1,0:T(8,128)(2,1)}), bf16[64,8,128]{2,1,0:T(8,128)(2,1)S(1)}, u32[]{:S(2)}, u32[]{:S(2)}) async-start(bf16[64,8,128]{2,1,0:T(8,128)(2,1)} %states.1), calls=%async_computation | async-start | bytes 262144 | tf_op jit(solution)/shard_map/all_to_all | solution.py:118
  43.5 0.7 copy-start.1
  45.9 17.3 %all-to-all-start.1 = ((bf16[64,8,128]{2,1,0:T(8,128)(2,1)}), bf16[64,8,128]{2,1,0:T(8,128)(2,1)S(1)}, u32[]{:S(2)}, u32[]{:S(2)}) async-start(bf16[64,8,128]{2,1,0:T(8,128)(2,1)} %scan.1), calls=%async_computation.1 | async-start | bytes 262144 | tf_op jit(solution)/shard_map/all_to_all | solution.py:126
  52.0 270.3 %reduce-scatter.2.cloned.1.call-start = ((), (), s32[]{:S(2)}) async-start(), calls=%async_computation.3 | async-start | bytes 2129920 | tf_op jit(solution)/shard_map/reduce_scatter | solution.py:148
  63.2 0.6 copy-start
Sparse Core Ops, SparseCore 0:
  71.9 250.3 reduce-scatter.1

commit v2 on v1

--- a/solution.py
+++ b/solution.py
@@ -10,6 +10,7 @@
 
 DH = 128
 CTX = ("ctx_0", "ctx_1")
+MESH_AXES = CTX + ("head",)
 F32 = jnp.float32
 BF16 = jnp.bfloat16
 
@@ -77,8 +78,10 @@
     return st_ref[at : at + rows].astype(F32).reshape(DH, DH).astype(BF16)
 
 
-def weights_kernel(scale, acts_ref, k_ref, loc_ref, st_ref, dv_ref, w_ref, dvs_ref):
-    @pl.when(pl.program_id(0) == 0)
+def weights_kernel(scale, core_ref, acts_ref, k_ref, loc_ref, st_ref, dv_ref, w_ref, dvs_ref):
+    i = pl.program_id(0)
+
+    @pl.when(i == 0)
     def _():
         for h in range(k_ref.shape[1] // DH):
             at = slice(h * DH, (h + 1) * DH)
@@ -87,7 +90,16 @@
             dvs_ref[:, at] = dvv.astype(BF16)
         dv_ref[...] = dvs_ref[...]
 
-    w_ref[...] = dot(acts_ref[...], dvs_ref[...], 0, 0).astype(w_ref.dtype)
+    part = dot(acts_ref[...], dvs_ref[...], 0, 0)
+    part = part.reshape((w_ref.shape[0],) + w_ref.shape[2:]).astype(w_ref.dtype)
+
+    @pl.when(core_ref[0] == 0)
+    def _():
+        w_ref[i] = part
+
+    @pl.when(core_ref[0] == 1)
+    def _():
+        w_ref[:, i] = part
 
 
 def back_kernel(scale, q_ref, k_ref, v_ref, o_ref, lq_ref, lk_ref, st_ref, dq_ref, dk_ref):
@@ -103,6 +115,24 @@
             out[:, at] = (factor * (grad - unit * inner)).astype(BF16)
 
 
+def core_groups(nx, nz, nh):
+    along_x, along_z = [], []
+    for h in range(nh):
+        for z in range(nz):
+            along_x.append([(x * nz + z) * nh + h for x in range(nx)])
+        for x in range(nx):
+            along_z.append([(x * nz + z) * nh + h for z in range(nz)])
+    even = lambda groups: [g for g in groups if g[0] % 2 == 0]
+    odd = lambda groups: [g for g in groups if g[0] % 2 == 1]
+    return even(along_x) + odd(along_z), even(along_z) + odd(along_x)
+
+
+def exchange(v, groups):
+    return lax.all_to_all(
+        v, MESH_AXES, split_axis=0, concat_axis=0, axis_index_groups=groups, tiled=True
+    )
+
+
 def shape(dims, dtype):
     return jax.ShapeDtypeStruct(dims, dtype)
 
@@ -113,7 +143,7 @@
     scale = float(toks * nblocks) ** (-0.5)
     pieces = 2 * width // 8
     st = pl.pallas_call(
-        states_kernel, out_shape=shape((pieces, 8, DH), BF16), name="states"
+        states_kernel, out_shape=shape((pieces, 8, DH), F32), name="states"
     )(queries, keys, values, out_grad)
     received = lax.all_to_all(st, CTX, split_axis=0, concat_axis=0, tiled=True)
     back = (lax.axis_index(CTX) >= nblocks // 2).astype(jnp.int32).reshape(1)
@@ -129,29 +159,37 @@
         functools.partial(local_kernel, scale), out_shape=(part, part, part), name="local"
     )(queries, keys, values, out_grad)
     rows = acts.shape[1]
-    step = 512
+    nx, nz, nh = (lax.axis_size(a) for a in MESH_AXES)
+    step = rows // nx
+    own = rows // nblocks
+    core = (lax.axis_index("head") % 2).astype(jnp.int32).reshape(1)
     whole = lambda *dims: pl.BlockSpec(dims, lambda i: (0,) * len(dims))
     dv_out, w = pl.pallas_call(
         functools.partial(weights_kernel, scale),
-        grid=(rows // step,),
+        grid=(nx,),
         in_specs=[
+            pl.BlockSpec(memory_space=pltpu.SMEM),
             pl.BlockSpec((toks, step), lambda i: (0, i)),
             whole(toks, width),
             whole(toks, width),
             whole(pieces, 8, DH),
         ],
-        out_specs=(whole(toks, width), pl.BlockSpec((step, width), lambda i: (i, 0))),
-        out_shape=(shape((toks, width), BF16), shape((rows, width), BF16)),
+        out_specs=(whole(toks, width), whole(nx, nz, own, width)),
+        out_shape=(shape((toks, width), BF16), shape((nx, nz, own, width), BF16)),
         scratch_shapes=[pltpu.VMEM((toks, width), BF16)],
         name="weights",
-    )(acts, keys, lv, low)
-    wv = lax.psum_scatter(w, CTX, scatter_dimension=0, tiled=True)
+    )(core, acts, keys, lv, low)
+    first, second = core_groups(nx, nz, nh)
+    got = exchange(w, first)
+    got = jnp.sum(got.astype(F32), axis=0).astype(BF16)
+    got = exchange(got, second)
+    wv = jnp.sum(got.astype(F32), axis=0)
     dq_out, dk_out = pl.pallas_call(
         functools.partial(back_kernel, scale),
         out_shape=(shape((toks, width), BF16),) * 2,
         name="back",
     )(queries, keys, values, out_grad, lq, lk, low)
-    return dq_out, dk_out, dv_out, wv.astype(F32)
+    return dq_out, dk_out, dv_out, wv
 
 
 def solution(mesh):

time: 331 us -> 119 us (0.36)
  the two profiles are of different devices: /device:TPU:4 before, /device:TPU:96 now
where the time goes in v2:
time: 119 us
  blocking collectives  33.6 us (28%)
  waiting for transfers between devices  31 us (26%)
  starting transfers between devices  30.6 us (26%)
  Pallas kernels  19.6 us (16%)
  other arithmetic  1.78 us (1%)
  local copies, waits for them, and re-layouts  1.35 us (1%)
    all_to_all x1, blocking collectives, exchange(): lax.all_to_all(v, MESH_AXES, split_axis=0, concat_axis=0, axis_index_grou...  33.6 us
    all_to_all x1, starting transfers between devices, on_device(): received = lax.all_to_all(st, CTX, split_axis=0, concat_axis=0, tiled=True)  22.6 us
    all_to_all x1, waiting for transfers between devices, on_device(): received = lax.all_to_all(st, CTX, split_axis=0, concat_axis=0, tiled=True)  14.9 us
    all_to_all x1, waiting for transfers between devices, on_device(): low = lax.all_to_all(answers, CTX, split_axis=0, concat_axis=0, tiled=True)  8.69 us
    pallas_call x1, Pallas kernels, on_device(): pl.pallas_call(functools.partial(weights_kernel, scale), grid=(nx,), in_s...  8.3 us
    all_to_all x1, waiting for transfers between devices, exchange(): lax.all_to_all(v, MESH_AXES, split_axis=0, concat_axis=0, axis_index_grou...  7.41 us
    all_to_all x1, starting transfers between devices, on_device(): low = lax.all_to_all(answers, CTX, split_axis=0, concat_axis=0, tiled=True)  4.62 us
    pallas_call x1, Pallas kernels, on_device(): pl.pallas_call(functools.partial(local_kernel, scale), out_shape=(part, p...  4.01 us
  transfers between devices with their start and end apart: 3, of which 3 were waited for; matrix products, arithmetic and copies ran while one was open for 0% of the time, Pallas kernels for 6%

profile of v2, /device:TPU:96, one launch (start us, length us, event | category | flops | bytes accessed | tf_op | source)
XLA Modules:
  0.0 118.7 jit_solution(10364279005685760892)
XLA Ops:
  0.6 2.6 %states.1 = f32[64,8,128]{2,1,0:T(8,128)} custom-call(bf16[512,256]{1,0:T(8,128)(2,1)} %q_ref.5, bf16[512,256]{1,0:T(8,128)(2,1)} %k_ref.7, bf16[512,256]{1,0:T(8,128)(2,1)} %v_ref.5, bf16[512,256]{1,0:T(8,128)(2,1)} %o_ref.5), custom_call_target="tpu_custom_call" | custom-call | tf_op jit(solution)/shard_map/states/pallas_call | solution.py:145
  3.2 22.6 %all-to-all-start = ((f32[64,8,128]{2,1,0:T(8,128)}), f32[64,8,128]{2,1,0:T(8,128)S(1)}, u32[]{:S(2)}, u32[]{:S(2)}) async-start(f32[64,8,128]{2,1,0:T(8,128)} %states.1), calls=%async_computation | async-start | bytes 524288 | tf_op jit(solution)/shard_map/all_to_all | solution.py:148
  25.8 14.9 %all-to-all-done.r_ref = f32[64,8,128]{2,1,0:T(8,128)S(1)} async-done(((f32[64,8,128]{2,1,0:T(8,128)}), f32[64,8,128]{2,1,0:T(8,128)S(1)}, u32[]{:S(2)}, u32[]{:S(2)}) %all-to-all-start) | async-done | bytes 262176 | tf_op jit(solution)/shard_map/all_to_all | solution.py:148
  40.8 0.0 copy-start.1
  40.8 0.7 copy-done.1
  41.5 1.8 %scan.1 = bf16[64,8,128]{2,1,0:T(8,128)(2,1)} custom-call(s32[1]{0:T(128)} %bitcast.back_ref, f32[64,8,128]{2,1,0:T(8,128)} %copy-done.1), custom_call_target="tpu_custom_call" | custom-call | tf_op jit(solution)/shard_map/scan/pallas_call | solution.py:150
  43.2 4.6 %all-to-all-start.1 = ((bf16[64,8,128]{2,1,0:T(8,128)(2,1)}), bf16[64,8,128]{2,1,0:T(8,128)(2,1)S(1)}, u32[]{:S(2)}, u32[]{:S(2)}) async-start(bf16[64,8,128]{2,1,0:T(8,128)(2,1)} %scan.1), calls=%async_computation.1 | async-start | bytes 262144 | tf_op jit(solution)/shard_map/all_to_all | solution.py:156
  47.8 4.0 %local.1 = (f32[512,256]{1,0:T(8,128)}, f32[512,256]{1,0:T(8,128)}, f32[512,256]{1,0:T(8,128)}) custom-call(bf16[512,256]{1,0:T(8,128)(2,1)} %q_ref.5, bf16[512,256]{1,0:T(8,128)(2,1)} %k_ref.7, bf16[512,256]{1,0:T(8,128)(2,1)} %v_ref.5, bf16[512,256]{1,0:T(8,128)(2,1)} %o_ref.5), custom_call_target="tpu_custom_call" | custom-call | tf_op jit(solution)/shard_map/local/pallas_call | solution.py:158
  51.9 8.7 %all-to-all-done.1.st_ref = bf16[64,8,128]{2,1,0:T(8,128)(2,1)S(1)} async-done(((bf16[64,8,128]{2,1,0:T(8,128)(2,1)}), bf16[64,8,128]{2,1,0:T(8,128)(2,1)S(1)}, u32[]{:S(2)}, u32[]{:S(2)}) %all-to-all-start.1) | async-done | bytes 131104 | tf_op jit(solution)/shard_map/all_to_all | solution.py:156
  60.5 0.0 copy-start
  60.6 0.6 copy-done
  61.2 8.3 %weights.1 = (bf16[512,256]{1,0:T(8,128)(2,1)}, bf16[8,8,64,256]{3,2,1,0:T(8,128)(2,1)}) custom-call(s32[1]{0:T(128)} %bitcast.1.core_ref, bf16[512,4096]{1,0:T(8,128)(2,1)} %acts_ref.1, bf16[512,256]{1,0:T(8,128)(2,1)} %k_ref.7, f32[512,256]{1,0:T(8,128)} %get-tuple-element.15.loc_ref, bf16[64,8,128]{2,1,0:T(8,128)(2,1)} %copy-done), custom_call_target="tpu_custom_call" | custom-call | tf_op jit(solution)/shard_map/weights/pallas_call | solution.py:167
  69.5 33.6 %all_to_all.20 = bf16[8,8,64,256]{3,2,1,0:T(8,128)(2,1)S(1)} all-to-all(bf16[8,8,64,256]{3,2,1,0:T(8,128)(2,1)} %get-tuple-element.17), channel_id=1, replica_groups={{0,128,256,384,512,640,768,896},{16,144,272,400,528,656,784,912},{32,16..., dimensions={0} | all-to-all | bytes 4194304 | tf_op jit(solution)/shard_map/all_to_all | solution.py:131
  103.1 1.1 reduce_sum.21
  104.3 3.4 %all-to-all-start.3 = ((bf16[8,64,256]{2,1,0:T(8,128)(2,1)}), bf16[8,64,256]{2,1,0:T(8,128)(2,1)S(1)}, u32[]{:S(2)}, u32[]{:S(2)}) async-start(bf16[8,64,256]{2,1,0:T(8,128)(2,1)} %reduce_sum.21), calls=%async_computation.3 | async-start | bytes 524288 | tf_op jit(solution)/shard_map/all_to_all | solution.py:131
  107.7 3.0 %back.1 = (bf16[512,256]{1,0:T(8,128)(2,1)}, bf16[512,256]{1,0:T(8,128)(2,1)}) custom-call(bf16[512,256]{1,0:T(8,128)(2,1)} %q_ref.5, bf16[512,256]{1,0:T(8,128)(2,1)} %k_ref.7, bf16[512,256]{1,0:T(8,128)(2,1)} %v_ref.5, bf16[512,256]{1,0:T(8,128)(2,1)} %o_ref.5, f32[512,256]{1,0:T(8,128)} %get-tuple-element.11.lq_ref, f32[512,256]{1,0:T(8,128)} %get-tuple-element.12.lk_ref, ...), custom_call_target="tpu_custom_call" | custom-call | tf_op jit(solution)/shard_map/back/pallas_call | solution.py:187
  110.7 7.4 %all-to-all-done.3 = bf16[8,64,256]{2,1,0:T(8,128)(2,1)S(1)} async-done(((bf16[8,64,256]{2,1,0:T(8,128)(2,1)}), bf16[8,64,256]{2,1,0:T(8,128)(2,1)S(1)}, u32[]{:S(2)}, u32[]{:S(2)}) %all-to-all-start.3) | async-done | bytes 262176 | tf_op jit(solution)/shard_map/all_to_all | solution.py:131
  118.1 0.7 convert_reduce_fusion
Async XLA Ops:
  3.2 37.5 %all-to-all-start = ((f32[64,8,128]{2,1,0:T(8,128)}), f32[64,8,128]{2,1,0:T(8,128)S(1)}, u32[]{:S(2)}, u32[]{:S(2)}) async-start(f32[64,8,128]{2,1,0:T(8,128)} %states.1), calls=%async_computation | async-start | bytes 524288 | tf_op jit(solution)/shard_map/all_to_all | solution.py:148
  40.8 0.7 copy-start.1
  43.2 17.3 %all-to-all-start.1 = ((bf16[64,8,128]{2,1,0:T(8,128)(2,1)}), bf16[64,8,128]{2,1,0:T(8,128)(2,1)S(1)}, u32[]{:S(2)}, u32[]{:S(2)}) async-start(bf16[64,8,128]{2,1,0:T(8,128)(2,1)} %scan.1), calls=%async_computation.1 | async-start | bytes 262144 | tf_op jit(solution)/shard_map/all_to_all | solution.py:156
  60.5 0.7 copy-start
  104.3 13.8 %all-to-all-start.3 = ((bf16[8,64,256]{2,1,0:T(8,128)(2,1)}), bf16[8,64,256]{2,1,0:T(8,128)(2,1)S(1)}, u32[]{:S(2)}, u32[]{:S(2)}) async-start(bf16[8,64,256]{2,1,0:T(8,128)(2,1)} %reduce_sum.21), calls=%async_computation.3 | async-start | bytes 524288 | tf_op jit(solution)/shard_map/all_to_all | solution.py:131

commit v3 on v1

v3 whole, which is shorter than its diff:
```python
import functools

import jax
import jax.numpy as jnp
from jax import lax
from jax.experimental import pallas as pl
from jax.experimental.pallas import tpu as pltpu
from jax.sharding import Mesh
from jax.sharding import PartitionSpec as P

DH = 128
CTX = ("ctx_0", "ctx_1")
MESH_AXES = CTX + ("head",)
ROW_CUTS = (8, 8)
F32 = jnp.float32
BF16 = jnp.bfloat16


def dot(a, b, ca, cb):
    return lax.dot_general(a, b, (((ca,), (cb,)), ((), ())), preferred_element_type=F32)


def unit_of(block):
    full = block.astype(F32)
    factor = lax.rsqrt(jnp.sum(full * full, axis=-1, keepdims=True) + 1e-06)
    return full * factor, factor


def head(ref, h):
    return ref[:, h * DH : (h + 1) * DH]


def states_kernel(q_ref, k_ref, v_ref, o_ref, st_ref):
    kn = unit_of(k_ref[...])[0].astype(BF16)
    qn = unit_of(q_ref[...])[0].astype(BF16)
    st_ref[0] = dot(kn, v_ref[...], 0, 0).reshape(st_ref.shape[1:])
    st_ref[1] = dot(qn, o_ref[...], 0, 0).reshape(st_ref.shape[1:])


def scan_kernel(back_ref, r_ref, after_ref, out_ref):
    del after_ref
    n = r_ref.shape[0]
    back = back_ref[0]

    def step(i, acc):
        b = jnp.where(back == 1, n - 1 - i, i)
        out_ref[b] = acc.astype(out_ref.dtype)
        return acc + r_ref[b].astype(F32)

    lax.fori_loop(0, n, step, jnp.zeros(r_ref.shape[1:], F32), unroll=8)


def local_kernel(scale, q_ref, k_ref, v_ref, o_ref, dq_ref, dk_ref, dv_ref, kn_ref):
    toks, width = q_ref.shape
    mask = lax.broadcasted_iota(jnp.int32, (toks, toks), 0) >= lax.broadcasted_iota(
        jnp.int32, (toks, toks), 1
    )
    for h in range(width // DH):
        at = slice(h * DH, (h + 1) * DH)
        kn = unit_of(head(k_ref, h))[0].astype(BF16)
        kn_ref[:, at] = kn
        qn = unit_of(head(q_ref, h))[0].astype(BF16)
        v, o = head(v_ref, h), head(o_ref, h)
        attn = jnp.where(mask, dot(qn, kn, 1, 1) * scale, 0.0).astype(BF16)
        dv_ref[:, at] = dot(attn, o, 0, 0)
        scores = jnp.where(mask, dot(o, v, 1, 1) * scale, 0.0).astype(BF16)
        dq_ref[:, at] = dot(scores, kn, 1, 0)
        dk_ref[:, at] = dot(scores, qn, 0, 0)


def state(st_ref, kind, h):
    heads = st_ref.shape[0] // 2 // (DH // 8)
    rows = DH // 8
    at = (kind * heads + h) * rows
    return st_ref[at : at + rows].astype(F32).reshape(DH, DH).astype(BF16)


def turn_kernel(core_ref, acts_ref, out_ref):
    x = pl.program_id(0)
    nx = pl.num_programs(0)
    nz, own = ROW_CUTS[1], out_ref.shape[2]
    turned = acts_ref[...].T.reshape(nz, own, acts_ref.shape[0])
    for core in range(2):

        @pl.when(core_ref[0] == core)
        def _():
            for z in range(nz):
                near, far = place(lax.rem(x + nx - core, nx), (z + nz - core) % nz, nz)
                out_ref[near, far] = turned[z]


def weights_kernel(scale, turned_ref, kn_ref, loc_ref, st_ref, dv_ref, w_ref, dvs_ref):
    @pl.when(pl.program_id(0) == 0)
    def _():
        for h in range(kn_ref.shape[1] // DH):
            at = slice(h * DH, (h + 1) * DH)
            dvv = loc_ref[:, at] + scale * dot(head(kn_ref, h), state(st_ref, 1, h), 1, 0)
            dvs_ref[:, at] = dvv.astype(BF16)
        dv_ref[...] = dvs_ref[...]

    w_ref[...] = dot(turned_ref[...], dvs_ref[...], 1, 0).astype(w_ref.dtype)


def back_kernel(scale, q_ref, k_ref, v_ref, o_ref, lq_ref, lk_ref, st_ref, dq_ref, dk_ref):
    for h in range(q_ref.shape[1] // DH):
        at = slice(h * DH, (h + 1) * DH)
        for src, other, loc, kind, out in (
            (q_ref, o_ref, lq_ref, 0, dq_ref),
            (k_ref, v_ref, lk_ref, 1, dk_ref),
        ):
            unit, factor = unit_of(head(src, h))
            grad = loc[:, at] + scale * dot(head(other, h), state(st_ref, kind, h), 1, 1)
            inner = jnp.sum(unit * grad, axis=-1, keepdims=True)
            out[:, at] = (factor * (grad - unit * inner)).astype(BF16)


def place(x, z, nz):
    return x % 2 * 2 + z % 2, x // 2 * (nz // 2) + z // 2


def core_groups(nx, nz, nh):
    squares, likes = {}, {}
    for h in range(nh):
        core = h % 2
        for x in range(nx):
            for z in range(nz):
                near, far = place((x + nx - core) % nx, (z + nz - core) % nz, nz)
                device = (x * nz + z) * nh + h
                squares.setdefault((h, far), {})[near] = device
                likes.setdefault((h, near), {})[far] = device
    ordered = lambda groups: [[g[i] for i in range(len(g))] for g in groups.values()]
    return ordered(squares), ordered(likes)


def exchange(v, groups):
    return lax.all_to_all(
        v, MESH_AXES, split_axis=0, concat_axis=0, axis_index_groups=groups, tiled=True
    )


def shape(dims, dtype):
    return jax.ShapeDtypeStruct(dims, dtype)


def on_device(acts, queries, keys, values, out_grad):
    toks, width = queries.shape
    nblocks = lax.axis_size(CTX)
    scale = float(toks * nblocks) ** (-0.5)
    pieces = 2 * width // 8
    heads = width // DH
    of_head = pl.BlockSpec((toks, DH), lambda h: (0, h))
    st = pl.pallas_call(
        states_kernel,
        grid=(heads,),
        in_specs=[of_head] * 4,
        out_specs=pl.BlockSpec((2, DH // 8, 8, DH), lambda h: (0, h, 0, 0)),
        out_shape=shape((2, heads * DH // 8, 8, DH), F32),
        name="states",
    )(queries, keys, values, out_grad).reshape(pieces, 8, DH)
    rows = acts.shape[1]
    nx, nz, nh = (lax.axis_size(a) for a in MESH_AXES)
    step = rows // nx
    own = rows // nblocks
    core = (lax.axis_index("head") % 2).astype(jnp.int32).reshape(1)
    whole = lambda *dims: pl.BlockSpec(dims, lambda i: (0,) * len(dims))
    cut = (4, nblocks // 4, own)
    turned = pl.pallas_call(
        turn_kernel,
        grid=(nx,),
        in_specs=[
            pl.BlockSpec(memory_space=pltpu.SMEM),
            pl.BlockSpec((toks, step), lambda i: (0, i)),
        ],
        out_specs=whole(*cut, toks),
        out_shape=shape((*cut, toks), BF16),
        name="turn",
    )(core, acts)
    received = lax.all_to_all(st, CTX, split_axis=0, concat_axis=0, tiled=True)
    back = (lax.axis_index(CTX) >= nblocks // 2).astype(jnp.int32).reshape(1)
    answers = pl.pallas_call(
        scan_kernel,
        in_specs=[
            pl.BlockSpec(memory_space=pltpu.SMEM),
            pl.BlockSpec(memory_space=pltpu.VMEM),
            pl.BlockSpec(memory_space=pl.ANY),
        ],
        out_shape=shape((nblocks, 8, DH), BF16),
        name="scan",
    )(back, pltpu.with_memory_space_constraint(received, pltpu.VMEM), turned)
    low = lax.all_to_all(answers, CTX, split_axis=0, concat_axis=0, tiled=True)
    low = pltpu.with_memory_space_constraint(low, pltpu.VMEM)
    part = shape((toks, width), F32)
    lq, lk, lv, kn = pl.pallas_call(
        functools.partial(local_kernel, scale),
        out_shape=(part, part, part, shape((toks, width), BF16)),
        name="local",
    )(queries, keys, values, out_grad)
    dv_out, w = pl.pallas_call(
        functools.partial(weights_kernel, scale),
        grid=(rows // step,),
        in_specs=[
            pl.BlockSpec((step, toks), lambda i: (i, 0)),
            whole(toks, width),
            whole(toks, width),
            pl.BlockSpec(memory_space=pltpu.VMEM),
        ],
        out_specs=(whole(toks, width), pl.BlockSpec((step, width), lambda i: (i, 0))),
        out_shape=(shape((toks, width), BF16), shape((rows, width), BF16)),
        scratch_shapes=[pltpu.VMEM((toks, width), BF16)],
        name="weights",
    )(turned.reshape(rows, toks), kn, lv, low)
    w = w.reshape(*cut, width)
    first, second = core_groups(nx, nz, nh)
    got = exchange(w, first)
    got = jnp.sum(got.astype(F32), axis=0).astype(BF16)
    got = exchange(got, second)
    wv = jnp.sum(got.astype(F32), axis=0)
    dq_out, dk_out = pl.pallas_call(
        functools.partial(back_kernel, scale),
        in_specs=[pl.BlockSpec(memory_space=pltpu.VMEM)] * 7,
        out_shape=(shape((toks, width), BF16),) * 2,
        name="back",
    )(queries, keys, values, out_grad, lq, lk, low)
    return dq_out, dk_out, dv_out, wv


def solution(mesh):
    finer = Mesh(mesh.devices.reshape(*ROW_CUTS, mesh.shape["head"]), ("ctx_0", "ctx_1", "head"))
    return jax.shard_map(
        on_device,
        mesh=finer,
        in_specs=(P(CTX, None), P(CTX, "head"), P(CTX, "head"), P(CTX, "head"), P(CTX, "head")),
        out_specs=(P(CTX, "head"), P(CTX, "head"), P(CTX, "head"), P(CTX, "head")),
        check_vma=False,
    )
```

time: 331 us -> 113 us (0.34)
  the two profiles are of different devices: /device:TPU:4 before, /device:TPU:34 now
where the time goes in v3:
time: 113 us; the launch traced here: 112 us
  starting transfers between devices  32.7 us (29%)
  waiting for transfers between devices  31.5 us (28%)
  Pallas kernels  25.5 us (23%)
  blocking collectives  19.5 us (17%)
  other arithmetic  2.02 us (2%)
    all_to_all x1, starting transfers between devices, on_device(): received = lax.all_to_all(st, CTX, split_axis=0, concat_axis=0, tiled=True)  22.7 us
    all_to_all x1, blocking collectives, exchange(): lax.all_to_all(v, MESH_AXES, split_axis=0, concat_axis=0, axis_index_grou...  19.5 us
    all_to_all x1, waiting for transfers between devices, exchange(): lax.all_to_all(v, MESH_AXES, split_axis=0, concat_axis=0, axis_index_grou...  17.6 us
    all_to_all x1, waiting for transfers between devices, on_device(): low = lax.all_to_all(answers, CTX, split_axis=0, concat_axis=0, tiled=True)  7.62 us
    pallas_call x1, Pallas kernels, on_device(): pl.pallas_call(functools.partial(weights_kernel, scale), grid=(rows // st...  7.57 us
    pallas_call x1, Pallas kernels, on_device(): pl.pallas_call(turn_kernel, grid=(nx,), in_specs=[pl.BlockSpec(memory_spa...  7.46 us
    all_to_all x1, starting transfers between devices, on_device(): low = lax.all_to_all(answers, CTX, split_axis=0, concat_axis=0, tiled=True)  6.43 us
    all_to_all x1, waiting for transfers between devices, on_device(): received = lax.all_to_all(st, CTX, split_axis=0, concat_axis=0, tiled=True)  6.27 us
  transfers between devices with their start and end apart: 3, of which 3 were waited for; matrix products, arithmetic and copies ran while one was open for 0% of the time, Pallas kernels for 13%

profile of v3, /device:TPU:34, one launch (start us, length us, event | category | flops | bytes accessed | tf_op | source)
XLA Modules:
  0.0 111.8 jit_solution(17870009095066707424)
XLA Ops:
  0.6 2.7 %states.1 = f32[2,32,8,128]{3,2,1,0:T(8,128)} custom-call(bf16[512,256]{1,0:T(8,128)(2,1)} %q_ref.5, bf16[512,256]{1,0:T(8,128)(2,1)} %k_ref.5, bf16[512,256]{1,0:T(8,128)(2,1)} %v_ref.5, bf16[512,256]{1,0:T(8,128)(2,1)} %o_ref.5), custom_call_target="tpu_custom_call" | custom-call | tf_op jit(solution)/shard_map/states/pallas_call | solution.py:152
  3.3 22.7 %all-to-all-start = ((f32[64,8,128]{2,1,0:T(8,128)}), f32[64,8,128]{2,1,0:T(8,128)S(1)}, u32[]{:S(2)}, u32[]{:S(2)}) async-start(f32[64,8,128]{2,1,0:T(8,128)} %bitcast.7), calls=%async_computation | async-start | bytes 524288 | tf_op jit(solution)/shard_map/all_to_all | solution.py:178
  26.0 7.5 %turn.1.after_ref = bf16[4,16,64,512]{3,2,1,0:T(8,128)(2,1)} custom-call(s32[1]{0:T(128)} %bitcast.2.core_ref, bf16[512,4096]{1,0:T(8,128)(2,1)} %acts_ref.1), custom_call_target="tpu_custom_call" | custom-call | tf_op jit(solution)/shard_map/turn/pallas_call | solution.py:167
  33.5 6.3 %all-to-all-done.r_ref = f32[64,8,128]{2,1,0:T(8,128)S(1)} async-done(((f32[64,8,128]{2,1,0:T(8,128)}), f32[64,8,128]{2,1,0:T(8,128)S(1)}, u32[]{:S(2)}, u32[]{:S(2)}) %all-to-all-start) | async-done | bytes 262176 | tf_op jit(solution)/shard_map/all_to_all | solution.py:178
  39.8 0.8 scan.1
  40.6 6.4 %all-to-all-start.1 = ((bf16[64,8,128]{2,1,0:T(8,128)(2,1)}), bf16[64,8,128]{2,1,0:T(8,128)(2,1)S(1)}, u32[]{:S(2)}, u32[]{:S(2)}) async-start(bf16[64,8,128]{2,1,0:T(8,128)(2,1)} %scan.1), calls=%async_computation.1 | async-start | bytes 262144 | tf_op jit(solution)/shard_map/all_to_all | solution.py:190
  47.0 4.0 %local.1 = (f32[512,256]{1,0:T(8,128)}, f32[512,256]{1,0:T(8,128)}, f32[512,256]{1,0:T(8,128)}, bf16[512,256]{1,0:T(8,128)(2,1)}) custom-call(bf16[512,256]{1,0:T(8,128)(2,1)} %q_ref.5, bf16[512,256]{1,0:T(8,128)(2,1)} %k_ref.5, bf16[512,256]{1,0:T(8,128)(2,1)} %v_ref.5, bf16[512,256]{1,0:T(8,128)(2,1)} %o_ref.5), custom_call_target="tpu_custom_call" | custom-call | tf_op jit(solution)/shard_map/local/pallas_call | solution.py:193
  51.0 7.6 %all-to-all-done.1.st_ref = bf16[64,8,128]{2,1,0:T(8,128)(2,1)S(1)} async-done(((bf16[64,8,128]{2,1,0:T(8,128)(2,1)}), bf16[64,8,128]{2,1,0:T(8,128)(2,1)S(1)}, u32[]{:S(2)}, u32[]{:S(2)}) %all-to-all-start.1) | async-done | bytes 131104 | tf_op jit(solution)/shard_map/all_to_all | solution.py:190
  58.7 7.6 %weights.1 = (bf16[512,256]{1,0:T(8,128)(2,1)}, bf16[4096,256]{1,0:T(8,128)(2,1)}) custom-call(bf16[4096,512]{1,0:T(8,128)(2,1)} %bitcast.5, bf16[512,256]{1,0:T(8,128)(2,1)} %get-tuple-element.16.kn_ref, f32[512,256]{1,0:T(8,128)} %get-tuple-element.17.loc_ref, bf16[64,8,128]{2,1,0:T(8,128)(2,1)S(1)} %all-to-all-done.1.st_ref), custom_call_target="tpu_custom_call" | custom-call | tf_op jit(solution)/shard_map/weights/pallas_call | solution.py:198
  66.2 19.5 %all_to_all.20 = bf16[4,16,64,256]{3,2,1,0:T(8,128)(2,1)S(1)} all-to-all(bf16[4,16,64,256]{3,2,1,0:T(8,128)(2,1)} %bitcast.6), channel_id=1, replica_groups={{0,16,128,144},{32,48,160,176},{64,80,192,208},{96,112,224,240},{256,27..., dimensions={0} | all-to-all | bytes 4194304 | tf_op jit(solution)/shard_map/all_to_all | solution.py:136
  85.7 1.3 %reduce_sum.21 = bf16[16,64,256]{2,1,0:T(8,128)(2,1)} reduce(bf16[4,16,64,256]{3,2,1,0:T(8,128)(2,1)S(1)} %all_to_all.20, bf16[]{:T(256)} %constant.31.clone.1), dimensions={0}, to_apply=%region_0.1 | reduce | flops 786432 | bytes 2621442 | tf_op jit(solution)/shard_map/reduce_sum | solution.py:215
  87.0 3.6 %all-to-all-start.3 = ((bf16[16,64,256]{2,1,0:T(8,128)(2,1)}), bf16[16,64,256]{2,1,0:T(8,128)(2,1)S(1)}, u32[]{:S(2)}, u32[]{:S(2)}) async-start(bf16[16,64,256]{2,1,0:T(8,128)(2,1)} %reduce_sum.21), calls=%async_computation.3 | async-start | bytes 1048576 | tf_op jit(solution)/shard_map/all_to_all | solution.py:136
  90.6 3.0 %back.1 = (bf16[512,256]{1,0:T(8,128)(2,1)}, bf16[512,256]{1,0:T(8,128)(2,1)}) custom-call(bf16[512,256]{1,0:T(8,128)(2,1)} %q_ref.5, bf16[512,256]{1,0:T(8,128)(2,1)} %k_ref.5, bf16[512,256]{1,0:T(8,128)(2,1)} %v_ref.5, bf16[512,256]{1,0:T(8,128)(2,1)} %o_ref.5, f32[512,256]{1,0:T(8,128)} %get-tuple-element.12.lq_ref, f32[512,256]{1,0:T(8,128)} %get-tuple-element.13.lk_ref, ...), custom_call_target="tpu_custom_call" | custom-call | tf_op jit(solution)/shard_map/back/pallas_call | solution.py:218
  93.6 17.6 %all-to-all-done.3 = bf16[16,64,256]{2,1,0:T(8,128)(2,1)S(1)} async-done(((bf16[16,64,256]{2,1,0:T(8,128)(2,1)}), bf16[16,64,256]{2,1,0:T(8,128)(2,1)S(1)}, u32[]{:S(2)}, u32[]{:S(2)}) %all-to-all-start.3) | async-done | bytes 524320 | tf_op jit(solution)/shard_map/all_to_all | solution.py:136
  111.1 0.7 convert_reduce_fusion
Async XLA Ops:
  3.3 36.5 %all-to-all-start = ((f32[64,8,128]{2,1,0:T(8,128)}), f32[64,8,128]{2,1,0:T(8,128)S(1)}, u32[]{:S(2)}, u32[]{:S(2)}) async-start(f32[64,8,128]{2,1,0:T(8,128)} %bitcast.7), calls=%async_computation | async-start | bytes 524288 | tf_op jit(solution)/shard_map/all_to_all | solution.py:178
  40.6 18.1 %all-to-all-start.1 = ((bf16[64,8,128]{2,1,0:T(8,128)(2,1)}), bf16[64,8,128]{2,1,0:T(8,128)(2,1)S(1)}, u32[]{:S(2)}, u32[]{:S(2)}) async-start(bf16[64,8,128]{2,1,0:T(8,128)(2,1)} %scan.1), calls=%async_computation.1 | async-start | bytes 262144 | tf_op jit(solution)/shard_map/all_to_all | solution.py:190
  87.0 24.1 %all-to-all-start.3 = ((bf16[16,64,256]{2,1,0:T(8,128)(2,1)}), bf16[16,64,256]{2,1,0:T(8,128)(2,1)S(1)}, u32[]{:S(2)}, u32[]{:S(2)}) async-start(bf16[16,64,256]{2,1,0:T(8,128)(2,1)} %reduce_sum.21), calls=%async_computation.3 | async-start | bytes 1048576 | tf_op jit(solution)/shard_map/all_to_all | solution.py:136

commit v4 on v3

--- a/solution.py
+++ b/solution.py
@@ -12,6 +12,7 @@
 CTX = ("ctx_0", "ctx_1")
 MESH_AXES = CTX + ("head",)
 ROW_CUTS = (8, 8)
+IN_VMEM = pl.BlockSpec(memory_space=pltpu.VMEM)
 F32 = jnp.float32
 BF16 = jnp.bfloat16
 
@@ -89,16 +90,35 @@
                 out_ref[near, far] = turned[z]
 
 
-def weights_kernel(scale, turned_ref, kn_ref, loc_ref, st_ref, dv_ref, w_ref, dvs_ref):
-    @pl.when(pl.program_id(0) == 0)
-    def _():
-        for h in range(kn_ref.shape[1] // DH):
-            at = slice(h * DH, (h + 1) * DH)
-            dvv = loc_ref[:, at] + scale * dot(head(kn_ref, h), state(st_ref, 1, h), 1, 0)
-            dvs_ref[:, at] = dvv.astype(BF16)
-        dv_ref[...] = dvs_ref[...]
-
-    w_ref[...] = dot(turned_ref[...], dvs_ref[...], 1, 0).astype(w_ref.dtype)
+def weights_kernel(
+    scale, turned_ref, kn_ref, loc_ref, st_ref, dv_ref, w_ref, rows_ref, low_ref, sums_ref, come, go
+):
+    n = come.shape[0]
+    step = rows_ref.shape[0] // n
+    at_step = lambda i: pl.ds(i * step, step)
+    coming = [
+        pltpu.make_async_copy(turned_ref.at[at_step(i)], rows_ref.at[at_step(i)], come.at[i])
+        for i in range(n)
+    ]
+    going = [
+        pltpu.make_async_copy(sums_ref.at[at_step(i)], w_ref.at[at_step(i)], go.at[i])
+        for i in range(n)
+    ]
+    for copy in coming:
+        copy.start()
+    for h in range(kn_ref.shape[1] // DH):
+        at = slice(h * DH, (h + 1) * DH)
+        dvv = loc_ref[:, at] + scale * dot(head(kn_ref, h), state(st_ref, 1, h), 1, 0)
+        low_ref[:, at] = dvv.astype(BF16)
+    kept = pltpu.make_async_copy(low_ref, dv_ref, go.at[n])
+    kept.start()
+    for i in range(n):
+        coming[i].wait()
+        sums_ref[at_step(i)] = dot(rows_ref[at_step(i)], low_ref[...], 1, 0).astype(BF16)
+        going[i].start()
+    for copy in going:
+        copy.wait()
+    kept.wait()
 
 
 def back_kernel(scale, q_ref, k_ref, v_ref, o_ref, lq_ref, lk_ref, st_ref, dq_ref, dk_ref):
@@ -136,6 +156,10 @@
     return lax.all_to_all(
         v, MESH_AXES, split_axis=0, concat_axis=0, axis_index_groups=groups, tiled=True
     )
+
+
+def in_vmem(v):
+    return pltpu.with_memory_space_constraint(v, pltpu.VMEM)
 
 
 def shape(dims, dtype):
@@ -181,34 +205,35 @@
         scan_kernel,
         in_specs=[
             pl.BlockSpec(memory_space=pltpu.SMEM),
-            pl.BlockSpec(memory_space=pltpu.VMEM),
+            IN_VMEM,
             pl.BlockSpec(memory_space=pl.ANY),
         ],
         out_shape=shape((nblocks, 8, DH), BF16),
         name="scan",
-    )(back, pltpu.with_memory_space_constraint(received, pltpu.VMEM), turned)
+    )(back, in_vmem(received), turned)
     low = lax.all_to_all(answers, CTX, split_axis=0, concat_axis=0, tiled=True)
-    low = pltpu.with_memory_space_constraint(low, pltpu.VMEM)
+    low = in_vmem(low)
     part = shape((toks, width), F32)
     lq, lk, lv, kn = pl.pallas_call(
         functools.partial(local_kernel, scale),
-        out_shape=(part, part, part, shape((toks, width), BF16)),
+        out_shape=(part, part, pltpu.VMEM((toks, width), F32), pltpu.VMEM((toks, width), BF16)),
         name="local",
     )(queries, keys, values, out_grad)
+    anywhere = pl.BlockSpec(memory_space=pl.ANY)
     dv_out, w = pl.pallas_call(
         functools.partial(weights_kernel, scale),
-        grid=(rows // step,),
-        in_specs=[
-            pl.BlockSpec((step, toks), lambda i: (i, 0)),
-            whole(toks, width),
-            whole(toks, width),
-            pl.BlockSpec(memory_space=pltpu.VMEM),
+        in_specs=[anywhere, IN_VMEM, IN_VMEM, IN_VMEM],
+        out_specs=(anywhere, anywhere),
+        out_shape=(shape((toks, width), BF16), shape((rows, width), BF16)),
+        scratch_shapes=[
+            pltpu.VMEM((rows, toks), BF16),
+            pltpu.VMEM((toks, width), BF16),
+            pltpu.VMEM((rows, width), BF16),
+            pltpu.SemaphoreType.DMA((nx,)),
+            pltpu.SemaphoreType.DMA((nx + 1,)),
         ],
-        out_specs=(whole(toks, width), pl.BlockSpec((step, width), lambda i: (i, 0))),
-        out_shape=(shape((toks, width), BF16), shape((rows, width), BF16)),
-        scratch_shapes=[pltpu.VMEM((toks, width), BF16)],
         name="weights",
-    )(turned.reshape(rows, toks), kn, lv, low)
+    )(turned.reshape(rows, toks), in_vmem(kn), in_vmem(lv), low)
     w = w.reshape(*cut, width)
     first, second = core_groups(nx, nz, nh)
     got = exchange(w, first)
@@ -217,7 +242,7 @@
     wv = jnp.sum(got.astype(F32), axis=0)
     dq_out, dk_out = pl.pallas_call(
         functools.partial(back_kernel, scale),
-        in_specs=[pl.BlockSpec(memory_space=pltpu.VMEM)] * 7,
+        in_specs=[IN_VMEM] * 7,
         out_shape=(shape((toks, width), BF16),) * 2,
         name="back",
     )(queries, keys, values, out_grad, lq, lk, low)

time: 113 us -> 110 us (0.973)
  Pallas kernels: 25.5 us -> 23.1 us
    pallas_call x2, Pallas kernels: 10.5 us -> 8.23 us  [the longest x1 5.27 us: on_device(): pl.pallas_call(functools.partial(weights_kernel, scale), in_specs=[anywhe...]
where the time goes in v4:
time: 110 us
  starting transfers between devices  32.7 us (30%)
  waiting for transfers between devices  31.6 us (29%)
  Pallas kernels  23.1 us (21%)
  blocking collectives  19.5 us (18%)
  other arithmetic  2.02 us (2%)
    all_to_all x1, starting transfers between devices, on_device(): received = lax.all_to_all(st, CTX, split_axis=0, concat_axis=0, tiled=True)  22.7 us
    all_to_all x1, blocking collectives, exchange(): lax.all_to_all(v, MESH_AXES, split_axis=0, concat_axis=0, axis_index_grou...  19.5 us
    all_to_all x1, waiting for transfers between devices, exchange(): lax.all_to_all(v, MESH_AXES, split_axis=0, concat_axis=0, axis_index_grou...  17.6 us
    all_to_all x1, waiting for transfers between devices, on_device(): low = lax.all_to_all(answers, CTX, split_axis=0, concat_axis=0, tiled=True)  7.77 us
    pallas_call x1, Pallas kernels, on_device(): pl.pallas_call(turn_kernel, grid=(nx,), in_specs=[pl.BlockSpec(memory_spa...  7.46 us
    all_to_all x1, starting transfers between devices, on_device(): low = lax.all_to_all(answers, CTX, split_axis=0, concat_axis=0, tiled=True)  6.43 us
    all_to_all x1, waiting for transfers between devices, on_device(): received = lax.all_to_all(st, CTX, split_axis=0, concat_axis=0, tiled=True)  6.27 us
    pallas_call x1, Pallas kernels, on_device(): pl.pallas_call(functools.partial(weights_kernel, scale), in_specs=[anywhe...  5.27 us
  transfers between devices with their start and end apart: 3, of which 3 were waited for; matrix products, arithmetic and copies ran while one was open for 0% of the time, Pallas kernels for 13%

profile of v4, /device:TPU:34, one launch (start us, length us, event | category | flops | bytes accessed | tf_op | source)
XLA Modules:
  0.0 109.5 jit_solution(9355780914298163156)
XLA Ops:
  0.6 2.7 %states.1 = f32[2,32,8,128]{3,2,1,0:T(8,128)} custom-call(bf16[512,256]{1,0:T(8,128)(2,1)} %q_ref.5, bf16[512,256]{1,0:T(8,128)(2,1)} %k_ref.5, bf16[512,256]{1,0:T(8,128)(2,1)} %v_ref.5, bf16[512,256]{1,0:T(8,128)(2,1)} %o_ref.5), custom_call_target="tpu_custom_call" | custom-call | tf_op jit(solution)/shard_map/states/pallas_call | solution.py:176
  3.3 22.7 %all-to-all-start = ((f32[64,8,128]{2,1,0:T(8,128)}), f32[64,8,128]{2,1,0:T(8,128)S(1)}, u32[]{:S(2)}, u32[]{:S(2)}) async-start(f32[64,8,128]{2,1,0:T(8,128)} %bitcast.7), calls=%async_computation | async-start | bytes 524288 | tf_op jit(solution)/shard_map/all_to_all | solution.py:202
  26.0 7.5 %turn.1.after_ref = bf16[4,16,64,512]{3,2,1,0:T(8,128)(2,1)} custom-call(s32[1]{0:T(128)} %bitcast.2.core_ref, bf16[512,4096]{1,0:T(8,128)(2,1)} %acts_ref.1), custom_call_target="tpu_custom_call" | custom-call | tf_op jit(solution)/shard_map/turn/pallas_call | solution.py:191
  33.5 6.3 %all-to-all-done.r_ref = f32[64,8,128]{2,1,0:T(8,128)S(1)} async-done(((f32[64,8,128]{2,1,0:T(8,128)}), f32[64,8,128]{2,1,0:T(8,128)S(1)}, u32[]{:S(2)}, u32[]{:S(2)}) %all-to-all-start) | async-done | bytes 262176 | tf_op jit(solution)/shard_map/all_to_all | solution.py:202
  39.8 0.8 scan.1
  40.6 6.4 %all-to-all-start.1 = ((bf16[64,8,128]{2,1,0:T(8,128)(2,1)}), bf16[64,8,128]{2,1,0:T(8,128)(2,1)S(1)}, u32[]{:S(2)}, u32[]{:S(2)}) async-start(bf16[64,8,128]{2,1,0:T(8,128)(2,1)} %scan.1), calls=%async_computation.1 | async-start | bytes 262144 | tf_op jit(solution)/shard_map/all_to_all | solution.py:214
  47.0 3.9 %local.1 = (f32[512,256]{1,0:T(8,128)}, f32[512,256]{1,0:T(8,128)}, f32[512,256]{1,0:T(8,128)S(1)}, bf16[512,256]{1,0:T(8,128)(2,1)S(1)}) custom-call(bf16[512,256]{1,0:T(8,128)(2,1)} %q_ref.5, bf16[512,256]{1,0:T(8,128)(2,1)} %k_ref.5, bf16[512,256]{1,0:T(8,128)(2,1)} %v_ref.5, bf16[512,256]{1,0:T(8,128)(2,1)} %o_ref.5), custom_call_target="tpu_custom_call" | custom-call | tf_op jit(solution)/shard_map/local/pallas_call | solution.py:217
  50.9 7.8 %all-to-all-done.1.st_ref = bf16[64,8,128]{2,1,0:T(8,128)(2,1)S(1)} async-done(((bf16[64,8,128]{2,1,0:T(8,128)(2,1)}), bf16[64,8,128]{2,1,0:T(8,128)(2,1)S(1)}, u32[]{:S(2)}, u32[]{:S(2)}) %all-to-all-start.1) | async-done | bytes 131104 | tf_op jit(solution)/shard_map/all_to_all | solution.py:214
  58.7 5.3 %weights.1 = (bf16[512,256]{1,0:T(8,128)(2,1)}, bf16[4096,256]{1,0:T(8,128)(2,1)}) custom-call(bf16[4096,512]{1,0:T(8,128)(2,1)} %bitcast.5, bf16[512,256]{1,0:T(8,128)(2,1)S(1)} %get-tuple-element.16.kn_ref, f32[512,256]{1,0:T(8,128)S(1)} %get-tuple-element.17.loc_ref, bf16[64,8,128]{2,1,0:T(8,128)(2,1)S(1)} %all-to-all-done.1.st_ref), custom_call_target="tpu_custom_call" | custom-call | tf_op jit(solution)/shard_map/weights/pallas_call | solution.py:223
  63.9 19.5 %all_to_all.20 = bf16[4,16,64,256]{3,2,1,0:T(8,128)(2,1)S(1)} all-to-all(bf16[4,16,64,256]{3,2,1,0:T(8,128)(2,1)} %bitcast.6), channel_id=1, replica_groups={{0,16,128,144},{32,48,160,176},{64,80,192,208},{96,112,224,240},{256,27..., dimensions={0} | all-to-all | bytes 4194304 | tf_op jit(solution)/shard_map/all_to_all | solution.py:156
  83.4 1.3 %reduce_sum.21 = bf16[16,64,256]{2,1,0:T(8,128)(2,1)} reduce(bf16[4,16,64,256]{3,2,1,0:T(8,128)(2,1)S(1)} %all_to_all.20, bf16[]{:T(256)} %constant.31.clone.1), dimensions={0}, to_apply=%region_0.1 | reduce | flops 786432 | bytes 2621442 | tf_op jit(solution)/shard_map/reduce_sum | solution.py:240
  84.7 3.6 %all-to-all-start.3 = ((bf16[16,64,256]{2,1,0:T(8,128)(2,1)}), bf16[16,64,256]{2,1,0:T(8,128)(2,1)S(1)}, u32[]{:S(2)}, u32[]{:S(2)}) async-start(bf16[16,64,256]{2,1,0:T(8,128)(2,1)} %reduce_sum.21), calls=%async_computation.3 | async-start | bytes 1048576 | tf_op jit(solution)/shard_map/all_to_all | solution.py:156
  88.3 3.0 %back.1 = (bf16[512,256]{1,0:T(8,128)(2,1)}, bf16[512,256]{1,0:T(8,128)(2,1)}) custom-call(bf16[512,256]{1,0:T(8,128)(2,1)} %q_ref.5, bf16[512,256]{1,0:T(8,128)(2,1)} %k_ref.5, bf16[512,256]{1,0:T(8,128)(2,1)} %v_ref.5, bf16[512,256]{1,0:T(8,128)(2,1)} %o_ref.5, f32[512,256]{1,0:T(8,128)} %get-tuple-element.12.lq_ref, f32[512,256]{1,0:T(8,128)} %get-tuple-element.13.lk_ref, ...), custom_call_target="tpu_custom_call" | custom-call | tf_op jit(solution)/shard_map/back/pallas_call | solution.py:243
  91.3 17.6 %all-to-all-done.3 = bf16[16,64,256]{2,1,0:T(8,128)(2,1)S(1)} async-done(((bf16[16,64,256]{2,1,0:T(8,128)(2,1)}), bf16[16,64,256]{2,1,0:T(8,128)(2,1)S(1)}, u32[]{:S(2)}, u32[]{:S(2)}) %all-to-all-start.3) | async-done | bytes 524320 | tf_op jit(solution)/shard_map/all_to_all | solution.py:156
  108.8 0.7 convert_reduce_fusion
Async XLA Ops:
  3.3 36.5 %all-to-all-start = ((f32[64,8,128]{2,1,0:T(8,128)}), f32[64,8,128]{2,1,0:T(8,128)S(1)}, u32[]{:S(2)}, u32[]{:S(2)}) async-start(f32[64,8,128]{2,1,0:T(8,128)} %bitcast.7), calls=%async_computation | async-start | bytes 524288 | tf_op jit(solution)/shard_map/all_to_all | solution.py:202
  40.6 18.1 %all-to-all-start.1 = ((bf16[64,8,128]{2,1,0:T(8,128)(2,1)}), bf16[64,8,128]{2,1,0:T(8,128)(2,1)S(1)}, u32[]{:S(2)}, u32[]{:S(2)}) async-start(bf16[64,8,128]{2,1,0:T(8,128)(2,1)} %scan.1), calls=%async_computation.1 | async-start | bytes 262144 | tf_op jit(solution)/shard_map/all_to_all | solution.py:214
  84.7 24.1 %all-to-all-start.3 = ((bf16[16,64,256]{2,1,0:T(8,128)(2,1)}), bf16[16,64,256]{2,1,0:T(8,128)(2,1)S(1)}, u32[]{:S(2)}, u32[]{:S(2)}) async-start(bf16[16,64,256]{2,1,0:T(8,128)(2,1)} %reduce_sum.21), calls=%async_computation.3 | async-start | bytes 1048576 | tf_op jit(solution)/shard_map/all_to_all | solution.py:156

commit v5 on v4

--- a/solution.py
+++ b/solution.py
@@ -10,7 +10,6 @@
 
 DH = 128
 CTX = ("ctx_0", "ctx_1")
-MESH_AXES = CTX + ("head",)
 ROW_CUTS = (8, 8)
 IN_VMEM = pl.BlockSpec(memory_space=pltpu.VMEM)
 F32 = jnp.float32
@@ -76,18 +75,8 @@
     return st_ref[at : at + rows].astype(F32).reshape(DH, DH).astype(BF16)
 
 
-def turn_kernel(core_ref, acts_ref, out_ref):
-    x = pl.program_id(0)
-    nx = pl.num_programs(0)
-    nz, own = ROW_CUTS[1], out_ref.shape[2]
-    turned = acts_ref[...].T.reshape(nz, own, acts_ref.shape[0])
-    for core in range(2):
-
-        @pl.when(core_ref[0] == core)
-        def _():
-            for z in range(nz):
-                near, far = place(lax.rem(x + nx - core, nx), (z + nz - core) % nz, nz)
-                out_ref[near, far] = turned[z]
+def turn_kernel(acts_ref, out_ref):
+    out_ref[...] = acts_ref[...].T
 
 
 def weights_kernel(
@@ -134,30 +123,6 @@
             out[:, at] = (factor * (grad - unit * inner)).astype(BF16)
 
 
-def place(x, z, nz):
-    return x % 2 * 2 + z % 2, x // 2 * (nz // 2) + z // 2
-
-
-def core_groups(nx, nz, nh):
-    squares, likes = {}, {}
-    for h in range(nh):
-        core = h % 2
-        for x in range(nx):
-            for z in range(nz):
-                near, far = place((x + nx - core) % nx, (z + nz - core) % nz, nz)
-                device = (x * nz + z) * nh + h
-                squares.setdefault((h, far), {})[near] = device
-                likes.setdefault((h, near), {})[far] = device
-    ordered = lambda groups: [[g[i] for i in range(len(g))] for g in groups.values()]
-    return ordered(squares), ordered(likes)
-
-
-def exchange(v, groups):
-    return lax.all_to_all(
-        v, MESH_AXES, split_axis=0, concat_axis=0, axis_index_groups=groups, tiled=True
-    )
-
-
 def in_vmem(v):
     return pltpu.with_memory_space_constraint(v, pltpu.VMEM)
 
@@ -182,23 +147,16 @@
         name="states",
     )(queries, keys, values, out_grad).reshape(pieces, 8, DH)
     rows = acts.shape[1]
-    nx, nz, nh = (lax.axis_size(a) for a in MESH_AXES)
-    step = rows // nx
     own = rows // nblocks
-    core = (lax.axis_index("head") % 2).astype(jnp.int32).reshape(1)
-    whole = lambda *dims: pl.BlockSpec(dims, lambda i: (0,) * len(dims))
-    cut = (4, nblocks // 4, own)
+    steps = 8
     turned = pl.pallas_call(
         turn_kernel,
-        grid=(nx,),
-        in_specs=[
-            pl.BlockSpec(memory_space=pltpu.SMEM),
-            pl.BlockSpec((toks, step), lambda i: (0, i)),
-        ],
-        out_specs=whole(*cut, toks),
-        out_shape=shape((*cut, toks), BF16),
+        grid=(steps,),
+        in_specs=[pl.BlockSpec((toks, rows // steps), lambda i: (0, i))],
+        out_specs=pl.BlockSpec((rows // steps, toks), lambda i: (i, 0)),
+        out_shape=shape((rows, toks), BF16),
         name="turn",
-    )(core, acts)
+    )(acts)
     received = lax.all_to_all(st, CTX, split_axis=0, concat_axis=0, tiled=True)
     back = (lax.axis_index(CTX) >= nblocks // 2).astype(jnp.int32).reshape(1)
     answers = pl.pallas_call(
@@ -229,16 +187,14 @@
             pltpu.VMEM((rows, toks), BF16),
             pltpu.VMEM((toks, width), BF16),
             pltpu.VMEM((rows, width), BF16),
-            pltpu.SemaphoreType.DMA((nx,)),
-            pltpu.SemaphoreType.DMA((nx + 1,)),
+            pltpu.SemaphoreType.DMA((steps,)),
+            pltpu.SemaphoreType.DMA((steps + 1,)),
         ],
         name="weights",
-    )(turned.reshape(rows, toks), in_vmem(kn), in_vmem(lv), low)
-    w = w.reshape(*cut, width)
-    first, second = core_groups(nx, nz, nh)
-    got = exchange(w, first)
-    got = jnp.sum(got.astype(F32), axis=0).astype(BF16)
-    got = exchange(got, second)
+    )(turned, in_vmem(kn), in_vmem(lv), low)
+    got = lax.all_to_all(
+        w.reshape(nblocks, own, width), CTX, split_axis=0, concat_axis=0, tiled=True
+    )
     wv = jnp.sum(got.astype(F32), axis=0)
     dq_out, dk_out = pl.pallas_call(
         functools.partial(back_kernel, scale),

time: 110 us -> 124 us (1.13)
  the two profiles are of different devices: /device:TPU:34 before, /device:TPU:86 now
where the time goes in v5:
time: 124 us
  waiting for transfers between devices  62.8 us (51%)
  starting transfers between devices  36.4 us (29%)
  Pallas kernels  22.8 us (18%)
    all_to_all x1, waiting for transfers between devices, on_device(): lax.all_to_all(w.reshape(nblocks, own, width), CTX, split_axis=0, concat_...  50.3 us
    all_to_all x1, starting transfers between devices, on_device(): received = lax.all_to_all(st, CTX, split_axis=0, concat_axis=0, tiled=True)  22.7 us
    pallas_call x1, Pallas kernels, on_device(): pl.pallas_call(turn_kernel, grid=(steps,), in_specs=[pl.BlockSpec((toks,...  7.19 us
    all_to_all x1, starting transfers between devices, on_device(): lax.all_to_all(w.reshape(nblocks, own, width), CTX, split_axis=0, concat_...  6.96 us
    all_to_all x1, starting transfers between devices, on_device(): low = lax.all_to_all(answers, CTX, split_axis=0, concat_axis=0, tiled=True)  6.76 us
    all_to_all x1, waiting for transfers between devices, on_device(): low = lax.all_to_all(answers, CTX, split_axis=0, concat_axis=0, tiled=True)  6.51 us
    all_to_all x1, waiting for transfers between devices, on_device(): received = lax.all_to_all(st, CTX, split_axis=0, concat_axis=0, tiled=True)  5.94 us
    pallas_call x1, Pallas kernels, on_device(): pl.pallas_call(functools.partial(weights_kernel, scale), in_specs=[anywhe...  5.26 us
  transfers between devices with their start and end apart: 3, of which 3 were waited for; matrix products, arithmetic and copies ran while one was open for 0% of the time, Pallas kernels for 11%

profile of v5, /device:TPU:86, one launch (start us, length us, event | category | flops | bytes accessed | tf_op | source)
XLA Modules:
  0.0 123.6 jit_solution(12838986055948096375)
XLA Ops:
  0.6 2.7 %states.1 = f32[2,32,8,128]{3,2,1,0:T(8,128)} custom-call(bf16[512,256]{1,0:T(8,128)(2,1)} %q_ref.5, bf16[512,256]{1,0:T(8,128)(2,1)} %k_ref.5, bf16[512,256]{1,0:T(8,128)(2,1)} %v_ref.5, bf16[512,256]{1,0:T(8,128)(2,1)} %o_ref.5), custom_call_target="tpu_custom_call" | custom-call | tf_op jit(solution)/shard_map/states/pallas_call | solution.py:141
  3.3 22.7 %all-to-all-start = ((f32[64,8,128]{2,1,0:T(8,128)}), f32[64,8,128]{2,1,0:T(8,128)S(1)}, u32[]{:S(2)}, u32[]{:S(2)}) async-start(f32[64,8,128]{2,1,0:T(8,128)} %bitcast.4), calls=%async_computation | async-start | bytes 524288 | tf_op jit(solution)/shard_map/all_to_all | solution.py:160
  26.0 7.2 %turn.1.after_ref.turned_ref = bf16[4096,512]{1,0:T(8,128)(2,1)} custom-call(bf16[512,4096]{1,0:T(8,128)(2,1)} %acts_ref.1), custom_call_target="tpu_custom_call" | custom-call | tf_op jit(solution)/shard_map/turn/pallas_call | solution.py:152
  33.2 5.9 %all-to-all-done.r_ref = f32[64,8,128]{2,1,0:T(8,128)S(1)} async-done(((f32[64,8,128]{2,1,0:T(8,128)}), f32[64,8,128]{2,1,0:T(8,128)S(1)}, u32[]{:S(2)}, u32[]{:S(2)}) %all-to-all-start) | async-done | bytes 262176 | tf_op jit(solution)/shard_map/all_to_all | solution.py:160
  39.1 0.8 scan.1
  40.0 6.8 %all-to-all-start.1 = ((bf16[64,8,128]{2,1,0:T(8,128)(2,1)}), bf16[64,8,128]{2,1,0:T(8,128)(2,1)S(1)}, u32[]{:S(2)}, u32[]{:S(2)}) async-start(bf16[64,8,128]{2,1,0:T(8,128)(2,1)} %scan.1), calls=%async_computation.1 | async-start | bytes 262144 | tf_op jit(solution)/shard_map/all_to_all | solution.py:172
  46.7 3.9 %local.1 = (f32[512,256]{1,0:T(8,128)}, f32[512,256]{1,0:T(8,128)}, f32[512,256]{1,0:T(8,128)S(1)}, bf16[512,256]{1,0:T(8,128)(2,1)S(1)}) custom-call(bf16[512,256]{1,0:T(8,128)(2,1)} %q_ref.5, bf16[512,256]{1,0:T(8,128)(2,1)} %k_ref.5, bf16[512,256]{1,0:T(8,128)(2,1)} %v_ref.5, bf16[512,256]{1,0:T(8,128)(2,1)} %o_ref.5), custom_call_target="tpu_custom_call" | custom-call | tf_op jit(solution)/shard_map/local/pallas_call | solution.py:175
  50.6 6.5 %all-to-all-done.1.st_ref = bf16[64,8,128]{2,1,0:T(8,128)(2,1)S(1)} async-done(((bf16[64,8,128]{2,1,0:T(8,128)(2,1)}), bf16[64,8,128]{2,1,0:T(8,128)(2,1)S(1)}, u32[]{:S(2)}, u32[]{:S(2)}) %all-to-all-start.1) | async-done | bytes 131104 | tf_op jit(solution)/shard_map/all_to_all | solution.py:172
  57.1 5.3 %weights.1 = (bf16[512,256]{1,0:T(8,128)(2,1)}, bf16[4096,256]{1,0:T(8,128)(2,1)}) custom-call(bf16[4096,512]{1,0:T(8,128)(2,1)} %turn.1.after_ref.turned_ref, bf16[512,256]{1,0:T(8,128)(2,1)S(1)} %get-tuple-element.16.kn_ref, f32[512,256]{1,0:T(8,128)S(1)} %get-tuple-element.17.loc_ref, bf16[64,8,128]{2,1,0:T(8,128)(2,1)S(1)} %all-to-all-done.1.st_ref), custom_call_target="tpu_custom_call" | custom-call | tf_op jit(solution)/shard_map/weights/pallas_call | solution.py:181
  62.4 7.0 %all-to-all-start.2 = ((bf16[64,64,256]{2,1,0:T(8,128)(2,1)}), bf16[64,64,256]{2,1,0:T(8,128)(2,1)S(1)}, u32[]{:S(2)}, u32[]{:S(2)}) async-start(bf16[64,64,256]{2,1,0:T(8,128)(2,1)} %bitcast.3), calls=%async_computation.2 | async-start | bytes 4194304 | tf_op jit(solution)/shard_map/all_to_all | solution.py:195
  69.4 3.0 %back.1 = (bf16[512,256]{1,0:T(8,128)(2,1)}, bf16[512,256]{1,0:T(8,128)(2,1)}) custom-call(bf16[512,256]{1,0:T(8,128)(2,1)} %q_ref.5, bf16[512,256]{1,0:T(8,128)(2,1)} %k_ref.5, bf16[512,256]{1,0:T(8,128)(2,1)} %v_ref.5, bf16[512,256]{1,0:T(8,128)(2,1)} %o_ref.5, f32[512,256]{1,0:T(8,128)} %get-tuple-element.12.lq_ref, f32[512,256]{1,0:T(8,128)} %get-tuple-element.13.lk_ref, ...), custom_call_target="tpu_custom_call" | custom-call | tf_op jit(solution)/shard_map/back/pallas_call | solution.py:199
  72.3 50.3 %all-to-all-done.2 = bf16[64,64,256]{2,1,0:T(8,128)(2,1)S(1)} async-done(((bf16[64,64,256]{2,1,0:T(8,128)(2,1)}), bf16[64,64,256]{2,1,0:T(8,128)(2,1)S(1)}, u32[]{:S(2)}, u32[]{:S(2)}) %all-to-all-start.2) | async-done | bytes 2097184 | tf_op jit(solution)/shard_map/all_to_all | solution.py:195
  122.7 0.9 convert_reduce_fusion
Async XLA Ops:
  3.3 35.8 %all-to-all-start = ((f32[64,8,128]{2,1,0:T(8,128)}), f32[64,8,128]{2,1,0:T(8,128)S(1)}, u32[]{:S(2)}, u32[]{:S(2)}) async-start(f32[64,8,128]{2,1,0:T(8,128)} %bitcast.4), calls=%async_computation | async-start | bytes 524288 | tf_op jit(solution)/shard_map/all_to_all | solution.py:160
  40.0 17.2 %all-to-all-start.1 = ((bf16[64,8,128]{2,1,0:T(8,128)(2,1)}), bf16[64,8,128]{2,1,0:T(8,128)(2,1)S(1)}, u32[]{:S(2)}, u32[]{:S(2)}) async-start(bf16[64,8,128]{2,1,0:T(8,128)(2,1)} %scan.1), calls=%async_computation.1 | async-start | bytes 262144 | tf_op jit(solution)/shard_map/all_to_all | solution.py:172
  62.4 60.3 %all-to-all-start.2 = ((bf16[64,64,256]{2,1,0:T(8,128)(2,1)}), bf16[64,64,256]{2,1,0:T(8,128)(2,1)S(1)}, u32[]{:S(2)}, u32[]{:S(2)}) async-start(bf16[64,64,256]{2,1,0:T(8,128)(2,1)} %bitcast.3), calls=%async_computation.2 | async-start | bytes 4194304 | tf_op jit(solution)/shard_map/all_to_all | solution.py:195

commit v6 on v4

--- a/solution.py
+++ b/solution.py
@@ -76,22 +76,27 @@
     return st_ref[at : at + rows].astype(F32).reshape(DH, DH).astype(BF16)
 
 
-def turn_kernel(core_ref, acts_ref, out_ref):
+def turn_kernel(core_ref, acts_ref, kept_ref, out_ref):
     x = pl.program_id(0)
     nx = pl.num_programs(0)
     nz, own = ROW_CUTS[1], out_ref.shape[2]
+    half = out_ref.shape[0]
     turned = acts_ref[...].T.reshape(nz, own, acts_ref.shape[0])
     for core in range(2):
-
-        @pl.when(core_ref[0] == core)
-        def _():
-            for z in range(nz):
-                near, far = place(lax.rem(x + nx - core, nx), (z + nz - core) % nz, nz)
-                out_ref[near, far] = turned[z]
+        for z in range(nz):
+            near, far = place(lax.rem(x + nx - core, nx), (z + nz - core) % nz, nz)
+
+            @pl.when((core_ref[0] == core) & (near < half))
+            def _():
+                kept_ref[near, far] = turned[z]
+
+            @pl.when((core_ref[0] == core) & (near >= half))
+            def _():
+                out_ref[near - half, far] = turned[z]
 
 
 def weights_kernel(
-    scale, turned_ref, kn_ref, loc_ref, st_ref, dv_ref, w_ref, rows_ref, low_ref, sums_ref, come, go
+    scale, kept_ref, turned_ref, kn_ref, loc_ref, st_ref, dv_ref, w_ref, rows_ref, low_ref, sums_ref, come, go
 ):
     n = come.shape[0]
     step = rows_ref.shape[0] // n
@@ -102,7 +107,7 @@
     ]
     going = [
         pltpu.make_async_copy(sums_ref.at[at_step(i)], w_ref.at[at_step(i)], go.at[i])
-        for i in range(n)
+        for i in range(2 * n)
     ]
     for copy in coming:
         copy.start()
@@ -110,15 +115,19 @@
         at = slice(h * DH, (h + 1) * DH)
         dvv = loc_ref[:, at] + scale * dot(head(kn_ref, h), state(st_ref, 1, h), 1, 0)
         low_ref[:, at] = dvv.astype(BF16)
-    kept = pltpu.make_async_copy(low_ref, dv_ref, go.at[n])
-    kept.start()
-    for i in range(n):
-        coming[i].wait()
-        sums_ref[at_step(i)] = dot(rows_ref[at_step(i)], low_ref[...], 1, 0).astype(BF16)
+    keep = pltpu.make_async_copy(low_ref, dv_ref, go.at[2 * n])
+    keep.start()
+    for i in range(2 * n):
+        if i < n:
+            rows = kept_ref[at_step(i)]
+        else:
+            coming[i - n].wait()
+            rows = rows_ref[at_step(i - n)]
+        sums_ref[at_step(i)] = dot(rows, low_ref[...], 1, 0).astype(BF16)
         going[i].start()
     for copy in going:
         copy.wait()
-    kept.wait()
+    keep.wait()
 
 
 def back_kernel(scale, q_ref, k_ref, v_ref, o_ref, lq_ref, lk_ref, st_ref, dq_ref, dk_ref):
@@ -135,7 +144,11 @@
 
 
 def place(x, z, nz):
-    return x % 2 * 2 + z % 2, x // 2 * (nz // 2) + z // 2
+    flip = nz // 2
+    return (
+        (x + x // flip) % 2 * 2 + (z + z // flip) % 2,
+        x // 2 * (nz // 2) + z // 2,
+    )
 
 
 def core_groups(nx, nz, nh):
@@ -188,15 +201,16 @@
     core = (lax.axis_index("head") % 2).astype(jnp.int32).reshape(1)
     whole = lambda *dims: pl.BlockSpec(dims, lambda i: (0,) * len(dims))
     cut = (4, nblocks // 4, own)
-    turned = pl.pallas_call(
+    half = (cut[0] // 2,) + cut[1:] + (toks,)
+    kept, turned = pl.pallas_call(
         turn_kernel,
         grid=(nx,),
         in_specs=[
             pl.BlockSpec(memory_space=pltpu.SMEM),
             pl.BlockSpec((toks, step), lambda i: (0, i)),
         ],
-        out_specs=whole(*cut, toks),
-        out_shape=shape((*cut, toks), BF16),
+        out_specs=(IN_VMEM, whole(*half)),
+        out_shape=(pltpu.VMEM(half, BF16), shape(half, BF16)),
         name="turn",
     )(core, acts)
     received = lax.all_to_all(st, CTX, split_axis=0, concat_axis=0, tiled=True)
@@ -222,18 +236,18 @@
     anywhere = pl.BlockSpec(memory_space=pl.ANY)
     dv_out, w = pl.pallas_call(
         functools.partial(weights_kernel, scale),
-        in_specs=[anywhere, IN_VMEM, IN_VMEM, IN_VMEM],
+        in_specs=[IN_VMEM, anywhere, IN_VMEM, IN_VMEM, IN_VMEM],
         out_specs=(anywhere, anywhere),
         out_shape=(shape((toks, width), BF16), shape((rows, width), BF16)),
         scratch_shapes=[
-            pltpu.VMEM((rows, toks), BF16),
+            pltpu.VMEM((rows // 2, toks), BF16),
             pltpu.VMEM((toks, width), BF16),
             pltpu.VMEM((rows, width), BF16),
-            pltpu.SemaphoreType.DMA((nx,)),
+            pltpu.SemaphoreType.DMA((nx // 2,)),
             pltpu.SemaphoreType.DMA((nx + 1,)),
         ],
         name="weights",
-    )(turned.reshape(rows, toks), in_vmem(kn), in_vmem(lv), low)
+    )(in_vmem(kept.reshape(rows // 2, toks)), turned.reshape(rows // 2, toks), in_vmem(kn), in_vmem(lv), low)
     w = w.reshape(*cut, width)
     first, second = core_groups(nx, nz, nh)
     got = exchange(w, first)

time: 110 us -> 108 us (0.982)
  the two profiles are of different devices: /device:TPU:34 before, /device:TPU:48 now
where the time goes in v6:
time: 108 us; the launch traced here: 107 us
  starting transfers between devices  32.1 us (30%)
  waiting for transfers between devices  30.2 us (28%)
  Pallas kernels  22.8 us (21%)
  blocking collectives  19.1 us (18%)
  other arithmetic  2.02 us (2%)
    all_to_all x1, starting transfers between devices, on_device(): received = lax.all_to_all(st, CTX, split_axis=0, concat_axis=0, tiled=True)  22.6 us
    all_to_all x1, blocking collectives, exchange(): lax.all_to_all(v, MESH_AXES, split_axis=0, concat_axis=0, axis_index_grou...  19.1 us
    all_to_all x1, waiting for transfers between devices, exchange(): lax.all_to_all(v, MESH_AXES, split_axis=0, concat_axis=0, axis_index_grou...  14.6 us
    all_to_all x1, waiting for transfers between devices, on_device(): low = lax.all_to_all(answers, CTX, split_axis=0, concat_axis=0, tiled=True)  8.8 us
    pallas_call x1, Pallas kernels, on_device(): pl.pallas_call(turn_kernel, grid=(nx,), in_specs=[pl.BlockSpec(memory_spa...  8.1 us
    all_to_all x1, waiting for transfers between devices, on_device(): received = lax.all_to_all(st, CTX, split_axis=0, concat_axis=0, tiled=True)  6.81 us
    all_to_all x1, starting transfers between devices, on_device(): low = lax.all_to_all(answers, CTX, split_axis=0, concat_axis=0, tiled=True)  5.89 us
    pallas_call x1, Pallas kernels, on_device(): pl.pallas_call(functools.partial(weights_kernel, scale), in_specs=[IN_VME...  4.44 us
  transfers between devices with their start and end apart: 3, of which 3 were waited for; matrix products, arithmetic and copies ran while one was open for 0% of the time, Pallas kernels for 14%

profile of v6, /device:TPU:48, one launch (start us, length us, event | category | flops | bytes accessed | tf_op | source)
XLA Modules:
  0.0 107.0 jit_solution(3642794536267607290)
XLA Ops:
  0.6 2.7 %states.1 = f32[2,32,8,128]{3,2,1,0:T(8,128)} custom-call(bf16[512,256]{1,0:T(8,128)(2,1)} %q_ref.5, bf16[512,256]{1,0:T(8,128)(2,1)} %k_ref.5, bf16[512,256]{1,0:T(8,128)(2,1)} %v_ref.5, bf16[512,256]{1,0:T(8,128)(2,1)} %o_ref.5), custom_call_target="tpu_custom_call" | custom-call | tf_op jit(solution)/shard_map/states/pallas_call | solution.py:189
  3.3 22.6 %all-to-all-start = ((f32[64,8,128]{2,1,0:T(8,128)}), f32[64,8,128]{2,1,0:T(8,128)S(1)}, u32[]{:S(2)}, u32[]{:S(2)}) async-start(f32[64,8,128]{2,1,0:T(8,128)} %bitcast.9), calls=%async_computation | async-start | bytes 524288 | tf_op jit(solution)/shard_map/all_to_all | solution.py:216
  26.0 8.1 %turn.1 = (bf16[2,16,64,512]{3,2,1,0:T(8,128)(2,1)S(1)}, bf16[2,16,64,512]{3,2,1,0:T(8,128)(2,1)}) custom-call(s32[1]{0:T(128)} %bitcast.2.core_ref, bf16[512,4096]{1,0:T(8,128)(2,1)} %acts_ref.1), custom_call_target="tpu_custom_call" | custom-call | tf_op jit(solution)/shard_map/turn/pallas_call | solution.py:205
  34.1 6.8 %all-to-all-done.r_ref = f32[64,8,128]{2,1,0:T(8,128)S(1)} async-done(((f32[64,8,128]{2,1,0:T(8,128)}), f32[64,8,128]{2,1,0:T(8,128)S(1)}, u32[]{:S(2)}, u32[]{:S(2)}) %all-to-all-start) | async-done | bytes 262176 | tf_op jit(solution)/shard_map/all_to_all | solution.py:216
  40.9 0.8 scan.1
  41.7 5.9 %all-to-all-start.1 = ((bf16[64,8,128]{2,1,0:T(8,128)(2,1)}), bf16[64,8,128]{2,1,0:T(8,128)(2,1)S(1)}, u32[]{:S(2)}, u32[]{:S(2)}) async-start(bf16[64,8,128]{2,1,0:T(8,128)(2,1)} %scan.1), calls=%async_computation.1 | async-start | bytes 262144 | tf_op jit(solution)/shard_map/all_to_all | solution.py:228
  47.6 3.8 %local.1 = (f32[512,256]{1,0:T(8,128)}, f32[512,256]{1,0:T(8,128)}, f32[512,256]{1,0:T(8,128)S(1)}, bf16[512,256]{1,0:T(8,128)(2,1)S(1)}) custom-call(bf16[512,256]{1,0:T(8,128)(2,1)} %q_ref.5, bf16[512,256]{1,0:T(8,128)(2,1)} %k_ref.5, bf16[512,256]{1,0:T(8,128)(2,1)} %v_ref.5, bf16[512,256]{1,0:T(8,128)(2,1)} %o_ref.5), custom_call_target="tpu_custom_call" | custom-call | tf_op jit(solution)/shard_map/local/pallas_call | solution.py:231
  51.4 8.8 %all-to-all-done.1.st_ref = bf16[64,8,128]{2,1,0:T(8,128)(2,1)S(1)} async-done(((bf16[64,8,128]{2,1,0:T(8,128)(2,1)}), bf16[64,8,128]{2,1,0:T(8,128)(2,1)S(1)}, u32[]{:S(2)}, u32[]{:S(2)}) %all-to-all-start.1) | async-done | bytes 131104 | tf_op jit(solution)/shard_map/all_to_all | solution.py:228
  60.2 4.4 %weights.1 = (bf16[512,256]{1,0:T(8,128)(2,1)}, bf16[4096,256]{1,0:T(8,128)(2,1)}) custom-call(bf16[2048,512]{1,0:T(8,128)(2,1)S(1)} %bitcast.6, bf16[2048,512]{1,0:T(8,128)(2,1)} %bitcast.7, bf16[512,256]{1,0:T(8,128)(2,1)S(1)} %get-tuple-element.20.kn_ref, f32[512,256]{1,0:T(8,128)S(1)} %get-tuple-element.21.loc_ref, ...), custom_call_target="tpu_custom_call" | custom-call | tf_op jit(solution)/shard_map/weights/pallas_call | solution.py:237
  64.7 19.1 %all_to_all.20 = bf16[4,16,64,256]{3,2,1,0:T(8,128)(2,1)S(1)} all-to-all(bf16[4,16,64,256]{3,2,1,0:T(8,128)(2,1)} %bitcast.8), channel_id=1, replica_groups={{0,16,128,144},{32,48,160,176},{80,64,208,192},{112,96,240,224},{256,27..., dimensions={0} | all-to-all | bytes 4194304 | tf_op jit(solution)/shard_map/all_to_all | solution.py:169
  83.8 1.3 %reduce_sum.21 = bf16[16,64,256]{2,1,0:T(8,128)(2,1)} reduce(bf16[4,16,64,256]{3,2,1,0:T(8,128)(2,1)S(1)} %all_to_all.20, bf16[]{:T(256)} %constant.31.clone.1), dimensions={0}, to_apply=%region_0.1 | reduce | flops 786432 | bytes 2621442 | tf_op jit(solution)/shard_map/reduce_sum | solution.py:254
  85.1 3.6 %all-to-all-start.3 = ((bf16[16,64,256]{2,1,0:T(8,128)(2,1)}), bf16[16,64,256]{2,1,0:T(8,128)(2,1)S(1)}, u32[]{:S(2)}, u32[]{:S(2)}) async-start(bf16[16,64,256]{2,1,0:T(8,128)(2,1)} %reduce_sum.21), calls=%async_computation.3 | async-start | bytes 1048576 | tf_op jit(solution)/shard_map/all_to_all | solution.py:169
  88.7 3.0 %back.1 = (bf16[512,256]{1,0:T(8,128)(2,1)}, bf16[512,256]{1,0:T(8,128)(2,1)}) custom-call(bf16[512,256]{1,0:T(8,128)(2,1)} %q_ref.5, bf16[512,256]{1,0:T(8,128)(2,1)} %k_ref.5, bf16[512,256]{1,0:T(8,128)(2,1)} %v_ref.5, bf16[512,256]{1,0:T(8,128)(2,1)} %o_ref.5, f32[512,256]{1,0:T(8,128)} %get-tuple-element.14.lq_ref, f32[512,256]{1,0:T(8,128)} %get-tuple-element.15.lk_ref, ...), custom_call_target="tpu_custom_call" | custom-call | tf_op jit(solution)/shard_map/back/pallas_call | solution.py:257
  91.7 14.6 %all-to-all-done.3 = bf16[16,64,256]{2,1,0:T(8,128)(2,1)S(1)} async-done(((bf16[16,64,256]{2,1,0:T(8,128)(2,1)}), bf16[16,64,256]{2,1,0:T(8,128)(2,1)S(1)}, u32[]{:S(2)}, u32[]{:S(2)}) %all-to-all-start.3) | async-done | bytes 524320 | tf_op jit(solution)/shard_map/all_to_all | solution.py:169
  106.3 0.7 convert_reduce_fusion
Async XLA Ops:
  3.3 37.6 %all-to-all-start = ((f32[64,8,128]{2,1,0:T(8,128)}), f32[64,8,128]{2,1,0:T(8,128)S(1)}, u32[]{:S(2)}, u32[]{:S(2)}) async-start(f32[64,8,128]{2,1,0:T(8,128)} %bitcast.9), calls=%async_computation | async-start | bytes 524288 | tf_op jit(solution)/shard_map/all_to_all | solution.py:216
  41.7 18.5 %all-to-all-start.1 = ((bf16[64,8,128]{2,1,0:T(8,128)(2,1)}), bf16[64,8,128]{2,1,0:T(8,128)(2,1)S(1)}, u32[]{:S(2)}, u32[]{:S(2)}) async-start(bf16[64,8,128]{2,1,0:T(8,128)(2,1)} %scan.1), calls=%async_computation.1 | async-start | bytes 262144 | tf_op jit(solution)/shard_map/all_to_all | solution.py:228
  85.1 21.1 %all-to-all-start.3 = ((bf16[16,64,256]{2,1,0:T(8,128)(2,1)}), bf16[16,64,256]{2,1,0:T(8,128)(2,1)S(1)}, u32[]{:S(2)}, u32[]{:S(2)}) async-start(bf16[16,64,256]{2,1,0:T(8,128)(2,1)} %reduce_sum.21), calls=%async_computation.3 | async-start | bytes 1048576 | tf_op jit(solution)/shard_map/all_to_all | solution.py:169

commit v7 on v6

--- a/solution.py
+++ b/solution.py
@@ -34,8 +34,8 @@
 def states_kernel(q_ref, k_ref, v_ref, o_ref, st_ref):
     kn = unit_of(k_ref[...])[0].astype(BF16)
     qn = unit_of(q_ref[...])[0].astype(BF16)
-    st_ref[0] = dot(kn, v_ref[...], 0, 0).reshape(st_ref.shape[1:])
-    st_ref[1] = dot(qn, o_ref[...], 0, 0).reshape(st_ref.shape[1:])
+    st_ref[0] = dot(kn, v_ref[...], 0, 0).reshape(st_ref.shape[1:]).astype(BF16)
+    st_ref[1] = dot(qn, o_ref[...], 0, 0).reshape(st_ref.shape[1:]).astype(BF16)
 
 
 def scan_kernel(back_ref, r_ref, after_ref, out_ref):
@@ -191,7 +191,7 @@
         grid=(heads,),
         in_specs=[of_head] * 4,
         out_specs=pl.BlockSpec((2, DH // 8, 8, DH), lambda h: (0, h, 0, 0)),
-        out_shape=shape((2, heads * DH // 8, 8, DH), F32),
+        out_shape=shape((2, heads * DH // 8, 8, DH), BF16),
         name="states",
     )(queries, keys, values, out_grad).reshape(pieces, 8, DH)
     rows = acts.shape[1]

time: 108 us -> 108 us (level)
  waiting for transfers between devices: 30.2 us -> 28 us
  starting transfers between devices: 32.1 us -> 34.3 us
    all_to_all x1, waiting for transfers between devices: 6.81 us -> 4.59 us  [on_device(): received = lax.all_to_all(st, CTX, split_axis=0, concat_axis=0, tiled=True)]
    all_to_all x1, starting transfers between devices: 5.89 us -> 8.11 us  [on_device(): low = lax.all_to_all(answers, CTX, split_axis=0, concat_axis=0, tiled=True)]
where the time goes in v7:
time: 108 us; the launch traced here: 107 us
  starting transfers between devices  34.3 us (32%)
  waiting for transfers between devices  28 us (26%)
  Pallas kernels  22.8 us (21%)
  blocking collectives  19.1 us (18%)
  other arithmetic  2.02 us (2%)
    all_to_all x1, starting transfers between devices, on_device(): received = lax.all_to_all(st, CTX, split_axis=0, concat_axis=0, tiled=True)  22.6 us
    all_to_all x1, blocking collectives, exchange(): lax.all_to_all(v, MESH_AXES, split_axis=0, concat_axis=0, axis_index_grou...  19.1 us
    all_to_all x1, waiting for transfers between devices, exchange(): lax.all_to_all(v, MESH_AXES, split_axis=0, concat_axis=0, axis_index_grou...  14.6 us
    all_to_all x1, waiting for transfers between devices, on_device(): low = lax.all_to_all(answers, CTX, split_axis=0, concat_axis=0, tiled=True)  8.8 us
    all_to_all x1, starting transfers between devices, on_device(): low = lax.all_to_all(answers, CTX, split_axis=0, concat_axis=0, tiled=True)  8.11 us
    pallas_call x1, Pallas kernels, on_device(): pl.pallas_call(turn_kernel, grid=(nx,), in_specs=[pl.BlockSpec(memory_spa...  8.1 us
    all_to_all x1, waiting for transfers between devices, on_device(): received = lax.all_to_all(st, CTX, split_axis=0, concat_axis=0, tiled=True)  4.59 us
    pallas_call x1, Pallas kernels, on_device(): pl.pallas_call(functools.partial(weights_kernel, scale), in_specs=[IN_VME...  4.44 us
  transfers between devices with their start and end apart: 3, of which 3 were waited for; matrix products, arithmetic and copies ran while one was open for 0% of the time, Pallas kernels for 14%

profile of v7, /device:TPU:48, one launch (start us, length us, event | category | flops | bytes accessed | tf_op | source)
XLA Modules:
  0.0 106.9 jit_solution(816177810991558273)
XLA Ops:
  0.6 2.7 %states.1 = bf16[2,32,8,128]{3,2,1,0:T(8,128)(2,1)} custom-call(bf16[512,256]{1,0:T(8,128)(2,1)} %q_ref.5, bf16[512,256]{1,0:T(8,128)(2,1)} %k_ref.5, bf16[512,256]{1,0:T(8,128)(2,1)} %v_ref.5, bf16[512,256]{1,0:T(8,128)(2,1)} %o_ref.5), custom_call_target="tpu_custom_call" | custom-call | tf_op jit(solution)/shard_map/states/pallas_call | solution.py:189
  3.3 22.6 %all-to-all-start = ((bf16[64,8,128]{2,1,0:T(8,128)(2,1)}), bf16[64,8,128]{2,1,0:T(8,128)(2,1)S(1)}, u32[]{:S(2)}, u32[]{:S(2)}) async-start(bf16[64,8,128]{2,1,0:T(8,128)(2,1)} %bitcast.9), calls=%async_computation | async-start | bytes 262144 | tf_op jit(solution)/shard_map/all_to_all | solution.py:216
  25.9 8.1 %turn.1 = (bf16[2,16,64,512]{3,2,1,0:T(8,128)(2,1)S(1)}, bf16[2,16,64,512]{3,2,1,0:T(8,128)(2,1)}) custom-call(s32[1]{0:T(128)} %bitcast.2.core_ref, bf16[512,4096]{1,0:T(8,128)(2,1)} %acts_ref.1), custom_call_target="tpu_custom_call" | custom-call | tf_op jit(solution)/shard_map/turn/pallas_call | solution.py:205
  34.0 4.6 %all-to-all-done.r_ref = bf16[64,8,128]{2,1,0:T(8,128)(2,1)S(1)} async-done(((bf16[64,8,128]{2,1,0:T(8,128)(2,1)}), bf16[64,8,128]{2,1,0:T(8,128)(2,1)S(1)}, u32[]{:S(2)}, u32[]{:S(2)}) %all-to-all-start) | async-done | bytes 131104 | tf_op jit(solution)/shard_map/all_to_all | solution.py:216
  38.6 0.8 scan.1
  39.4 8.1 %all-to-all-start.1 = ((bf16[64,8,128]{2,1,0:T(8,128)(2,1)}), bf16[64,8,128]{2,1,0:T(8,128)(2,1)S(1)}, u32[]{:S(2)}, u32[]{:S(2)}) async-start(bf16[64,8,128]{2,1,0:T(8,128)(2,1)} %scan.1), calls=%async_computation.1 | async-start | bytes 262144 | tf_op jit(solution)/shard_map/all_to_all | solution.py:228
  47.5 3.8 %local.1 = (f32[512,256]{1,0:T(8,128)}, f32[512,256]{1,0:T(8,128)}, f32[512,256]{1,0:T(8,128)S(1)}, bf16[512,256]{1,0:T(8,128)(2,1)S(1)}) custom-call(bf16[512,256]{1,0:T(8,128)(2,1)} %q_ref.5, bf16[512,256]{1,0:T(8,128)(2,1)} %k_ref.5, bf16[512,256]{1,0:T(8,128)(2,1)} %v_ref.5, bf16[512,256]{1,0:T(8,128)(2,1)} %o_ref.5), custom_call_target="tpu_custom_call" | custom-call | tf_op jit(solution)/shard_map/local/pallas_call | solution.py:231
  51.4 8.8 %all-to-all-done.1.st_ref = bf16[64,8,128]{2,1,0:T(8,128)(2,1)S(1)} async-done(((bf16[64,8,128]{2,1,0:T(8,128)(2,1)}), bf16[64,8,128]{2,1,0:T(8,128)(2,1)S(1)}, u32[]{:S(2)}, u32[]{:S(2)}) %all-to-all-start.1) | async-done | bytes 131104 | tf_op jit(solution)/shard_map/all_to_all | solution.py:228
  60.2 4.4 %weights.1 = (bf16[512,256]{1,0:T(8,128)(2,1)}, bf16[4096,256]{1,0:T(8,128)(2,1)}) custom-call(bf16[2048,512]{1,0:T(8,128)(2,1)S(1)} %bitcast.6, bf16[2048,512]{1,0:T(8,128)(2,1)} %bitcast.7, bf16[512,256]{1,0:T(8,128)(2,1)S(1)} %get-tuple-element.20.kn_ref, f32[512,256]{1,0:T(8,128)S(1)} %get-tuple-element.21.loc_ref, ...), custom_call_target="tpu_custom_call" | custom-call | tf_op jit(solution)/shard_map/weights/pallas_call | solution.py:237
  64.6 19.1 %all_to_all.20 = bf16[4,16,64,256]{3,2,1,0:T(8,128)(2,1)S(1)} all-to-all(bf16[4,16,64,256]{3,2,1,0:T(8,128)(2,1)} %bitcast.8), channel_id=1, replica_groups={{0,16,128,144},{32,48,160,176},{80,64,208,192},{112,96,240,224},{256,27..., dimensions={0} | all-to-all | bytes 4194304 | tf_op jit(solution)/shard_map/all_to_all | solution.py:169
  83.8 1.3 %reduce_sum.21 = bf16[16,64,256]{2,1,0:T(8,128)(2,1)} reduce(bf16[4,16,64,256]{3,2,1,0:T(8,128)(2,1)S(1)} %all_to_all.20, bf16[]{:T(256)} %constant.31.clone.1), dimensions={0}, to_apply=%region_0.1 | reduce | flops 786432 | bytes 2621442 | tf_op jit(solution)/shard_map/reduce_sum | solution.py:254
  85.1 3.6 %all-to-all-start.3 = ((bf16[16,64,256]{2,1,0:T(8,128)(2,1)}), bf16[16,64,256]{2,1,0:T(8,128)(2,1)S(1)}, u32[]{:S(2)}, u32[]{:S(2)}) async-start(bf16[16,64,256]{2,1,0:T(8,128)(2,1)} %reduce_sum.21), calls=%async_computation.3 | async-start | bytes 1048576 | tf_op jit(solution)/shard_map/all_to_all | solution.py:169
  88.7 3.0 %back.1 = (bf16[512,256]{1,0:T(8,128)(2,1)}, bf16[512,256]{1,0:T(8,128)(2,1)}) custom-call(bf16[512,256]{1,0:T(8,128)(2,1)} %q_ref.5, bf16[512,256]{1,0:T(8,128)(2,1)} %k_ref.5, bf16[512,256]{1,0:T(8,128)(2,1)} %v_ref.5, bf16[512,256]{1,0:T(8,128)(2,1)} %o_ref.5, f32[512,256]{1,0:T(8,128)} %get-tuple-element.14.lq_ref, f32[512,256]{1,0:T(8,128)} %get-tuple-element.15.lk_ref, ...), custom_call_target="tpu_custom_call" | custom-call | tf_op jit(solution)/shard_map/back/pallas_call | solution.py:257
  91.6 14.6 %all-to-all-done.3 = bf16[16,64,256]{2,1,0:T(8,128)(2,1)S(1)} async-done(((bf16[16,64,256]{2,1,0:T(8,128)(2,1)}), bf16[16,64,256]{2,1,0:T(8,128)(2,1)S(1)}, u32[]{:S(2)}, u32[]{:S(2)}) %all-to-all-start.3) | async-done | bytes 524320 | tf_op jit(solution)/shard_map/all_to_all | solution.py:169
  106.2 0.7 convert_reduce_fusion
Async XLA Ops:
  3.3 35.3 %all-to-all-start = ((bf16[64,8,128]{2,1,0:T(8,128)(2,1)}), bf16[64,8,128]{2,1,0:T(8,128)(2,1)S(1)}, u32[]{:S(2)}, u32[]{:S(2)}) async-start(bf16[64,8,128]{2,1,0:T(8,128)(2,1)} %bitcast.9), calls=%async_computation | async-start | bytes 262144 | tf_op jit(solution)/shard_map/all_to_all | solution.py:216
  39.4 20.8 %all-to-all-start.1 = ((bf16[64,8,128]{2,1,0:T(8,128)(2,1)}), bf16[64,8,128]{2,1,0:T(8,128)(2,1)S(1)}, u32[]{:S(2)}, u32[]{:S(2)}) async-start(bf16[64,8,128]{2,1,0:T(8,128)(2,1)} %scan.1), calls=%async_computation.1 | async-start | bytes 262144 | tf_op jit(solution)/shard_map/all_to_all | solution.py:228
  85.1 21.1 %all-to-all-start.3 = ((bf16[16,64,256]{2,1,0:T(8,128)(2,1)}), bf16[16,64,256]{2,1,0:T(8,128)(2,1)S(1)}, u32[]{:S(2)}, u32[]{:S(2)}) async-start(bf16[16,64,256]{2,1,0:T(8,128)(2,1)} %reduce_sum.21), calls=%async_computation.3 | async-start | bytes 1048576 | tf_op jit(solution)/shard_map/all_to_all | solution.py:169
